TPU v7x, 32 devices: a whole 2x2x4 slice. The times are simulated.
32 devices in a mesh: tok: 4 (over x, core), head: 4 (over z), seq: 2 (over y).
Axes of the slice: x: 2, y: 2, z: 4, core: 2. Of those that a mesh axis runs over, the one named last changes fastest.
Arguments:
- queries: bfloat16 [2, 4096, 2048], P('seq', ('tok', 'head')), may hold values from -6 to 6
- keys: bfloat16 [2, 4096, 2048], P('seq', ('tok', 'head')), may hold values from -6 to 6
- values: bfloat16 [2, 4096, 2048], P('seq', ('tok', 'head')), may hold values from -6 to 6
- rates: float32 [2, 4, 4096], P('seq', 'head', 'tok'), may hold values from 0.00015625 to 0.0015625
- fast_one: float32 [4, 512, 512], P('head'), may hold values from -0.25 to 0.25
- fast_two: float32 [4, 512, 512], P('head'), may hold values from -0.25 to 0.25
- fast_three: float32 [4, 512, 512], P('head'), may hold values from -0.25 to 0.25
- grad_out: bfloat16 [2, 4096, 2048], P('seq', ('tok', 'head')), may hold values from -6 to 6
Outputs:
- grad_queries: bfloat16 [2, 4096, 2048], P('seq', ('tok', 'head'))
- grad_keys: bfloat16 [2, 4096, 2048], P('seq', ('tok', 'head'))
- grad_values: bfloat16 [2, 4096, 2048], P('seq', ('tok', 'head'))
- grad_rates: float32 [2, 4, 4096], P('seq', 'head', 'tok')
- grad_fast_one: float32 [4, 512, 512], P('head')
- grad_fast_two: float32 [4, 512, 512], P('head')
- grad_fast_three: float32 [4, 512, 512], P('head')
All inputs are finite; a program needn't handle non-finite values.
Results may differ from a plain program's by a relative error of at most 0.016.
Values may be sent and summed in bfloat16 or wider, within the bound.
No kernel may reach another device: no remote copies, remote signals or barrier semaphores. Data moves between devices by JAX's collectives and lax.ppermute only.
A program may use at most 128 MiB of HBM per device.

v0:
```python
import functools

import jax
import jax.numpy as jnp
from jax import lax
from jax.experimental import pallas as pl
from jax.experimental.pallas import tpu as pltpu
from jax.sharding import PartitionSpec as P


epsilon = 1e-06
bf16 = jnp.bfloat16
f32 = jnp.float32


def dot_nn(left, right):
    return lax.dot_general(left, right, (((1,), (0,)), ((), ())), preferred_element_type=f32)


def dot_tn(left, right):
    return lax.dot_general(left, right, (((0,), (0,)), ((), ())), preferred_element_type=f32)


def dot_nt(left, right):
    return lax.dot_general(left, right, (((1,), (1,)), ((), ())), preferred_element_type=f32)


def sigmoid(x):
    return 0.5 * jnp.tanh(0.5 * x) + 0.5


def columns(idx, half):
    own = pl.multiple_of(idx[1] * half, half)
    other = pl.multiple_of((1 - idx[1]) * half, half)
    return own, other


def emit_halves(idx, pairs, keep, send):
    half = keep.shape[2]
    own, other = columns(idx, half)
    for j, (left, right) in enumerate(pairs):
        send[j] = dot_tn(left[...], right[:, pl.ds(other, half)]).astype(bf16)
    for j, (left, right) in enumerate(pairs):
        keep[j] = dot_tn(left[...], right[:, pl.ds(own, half)])


def join_halves(idx, own_ref, other_ref, out):
    half = own_ref.shape[2]
    own, other = columns(idx, half)
    for j in range(3):
        out[j, :, pl.ds(own, half)] = own_ref[j]
        out[j, :, pl.ds(other, half)] = other_ref[j]


def piece_rate(idx, rate, piece, rows):
    return rate[pl.ds(pl.multiple_of((idx[0] ^ piece) * rows, rows), rows), :]


def cut_kernel(idx, left, right, *outs):
    width = outs[0].shape[2]
    for p, out in enumerate(outs):
        lanes = pl.ds(pl.multiple_of((idx[0] ^ p) * width, width), width)
        out[0] = left[:, lanes]
        out[1] = right[:, lanes]


def inner_kernel(count, idx, rate, w_one, w_two, w_three, *refs):
    pieces = refs[:count]
    keep, send, kb, tb, hb, d_one_b, d_three_b = refs[count:]
    rows = pieces[0].shape[1]
    for p in range(count):
        at = slice(p * rows, (p + 1) * rows)
        k = pieces[p][0]
        t = (-piece_rate(idx, rate, p, rows) * pieces[p][1].astype(f32)).astype(bf16)
        a_one = dot_nn(k, w_one[...])
        a_three = dot_nn(k, w_three[...])
        b = dot_nt(t, w_two[...])
        sq = sigmoid(a_one)
        swished = a_one * sq
        slope = sq * (1.0 + a_one * (1.0 - sq))
        kb[at] = k
        tb[at] = t
        hb[at] = (swished * a_three).astype(bf16)
        d_one_b[at] = (b * a_three * slope).astype(bf16)
        d_three_b[at] = (b * swished).astype(bf16)
    emit_halves(idx, ((kb, d_one_b), (hb, tb), (kb, d_three_b)), keep, send)


def factor_kernel(count, idx, rate, w_one, w_two, w_three, *refs):
    pieces = refs[:count]
    key_o, value_o, hid_o, d_one_o, d_three_o, f_one, f_two, f_three, f_four = refs[count:]
    for p in range(count):
        k = pieces[p][0]
        v = pieces[p][1]
        t = (-piece_rate(idx, rate, p, k.shape[0]) * v.astype(f32)).astype(bf16)
        a_one = dot_nn(k, w_one[...])
        a_three = dot_nn(k, w_three[...])
        b = dot_nt(t, w_two[...])
        sq = sigmoid(a_one)
        swished = a_one * sq
        slope = sq * (1.0 + a_one * (1.0 - sq))
        slope_two = sq * (1.0 - sq) * (2.0 + a_one * (1.0 - 2.0 * sq))
        key_o[p] = k
        value_o[p] = v
        hid_o[p] = (swished * a_three).astype(bf16)
        d_one_o[p] = (b * a_three * slope).astype(bf16)
        d_three_o[p] = (b * swished).astype(bf16)
        f_one[p] = (a_three * slope).astype(bf16)
        f_two[p] = swished.astype(bf16)
        f_three[p] = (b * slope).astype(bf16)
        f_four[p] = (b * a_three * slope_two).astype(bf16)


def normalize_kernel(mine, theirs, weight, update, stats, new):
    w = weight[0]
    u = w - (mine[0].astype(f32) + theirs[0].astype(f32))
    ref_norm = jnp.sqrt(jnp.sum(w * w, axis=0, keepdims=True) + epsilon)
    upd_norm = jnp.sqrt(jnp.sum(u * u, axis=0, keepdims=True) + epsilon)
    update[0] = u
    stats[0, 0:1, :] = ref_norm
    stats[0, 1:2, :] = upd_norm
    new[0] = (u * (ref_norm / upd_norm)).astype(bf16)


def outer_piece(q, e, y, at, qb, eb, mb, d_one_b, d_three_b):
    c_one = dot_nn(q, y[0])
    c_three = dot_nn(q, y[2])
    dm = dot_nt(e, y[1])
    sq = sigmoid(c_one)
    swished = c_one * sq
    slope = sq * (1.0 + c_one * (1.0 - sq))
    qb[at] = q
    eb[at] = e
    mb[at] = (swished * c_three).astype(bf16)
    d_one_b[at] = (dm * c_three * slope).astype(bf16)
    d_three_b[at] = (dm * swished).astype(bf16)


def apply_early_kernel(count, idx, y_own, y_other, *refs):
    pieces = refs[:count]
    qb, eb, mb, d_one_b, d_three_b, y = refs[count:]
    join_halves(idx, y_own, y_other, y)
    rows = pieces[0].shape[1]
    for p in range(count):
        at = slice(p * rows, (p + 1) * rows)
        outer_piece(pieces[p][0], pieces[p][1], y, at, qb, eb, mb, d_one_b, d_three_b)


def apply_late_kernel(count, idx, y_own, y_other, *refs):
    pieces, early = refs[:count], refs[count : count + 5]
    keep, send, d_one_b, d_three_b, qb, eb, mb, y = refs[count + 5 :]
    join_halves(idx, y_own, y_other, y)
    rows = pieces[0].shape[1]
    start = early[0].shape[0]
    for source, target in zip(early, (qb, eb, mb, d_one_b, d_three_b)):
        target[:start] = source[...]
    for p in range(count):
        at = slice(start + p * rows, start + (p + 1) * rows)
        outer_piece(pieces[p][0], pieces[p][1], y, at, qb, eb, mb, d_one_b, d_three_b)
    emit_halves(idx, ((qb, d_one_b), (mb, eb), (qb, d_three_b)), keep, send)


def query_kernel(count, idx, y_own, y_other, d_one, d_three, *refs):
    grads, y = refs[:count], refs[count]
    join_halves(idx, y_own, y_other, y)
    rows = grads[0].shape[0]
    for p in range(count):
        at = slice(p * rows, (p + 1) * rows)
        grads[p][...] = (dot_nt(d_one[at], y[0]) + dot_nt(d_three[at], y[2])).astype(bf16)


def adjoint_kernel(mine, theirs, update, stats, cot, moments):
    u = update[0]
    ref_norm = stats[0, 0:1, :]
    upd_norm = stats[0, 1:2, :]
    dy = mine[0].astype(f32) + theirs[0].astype(f32)
    moment = jnp.sum(dy * u, axis=0, keepdims=True)
    factor = ref_norm / upd_norm
    cot[0] = (u * (factor * moment / (upd_norm * upd_norm)) - factor * dy).astype(bf16)
    moments[0] = moment


def double_kernel(base, count, idx, rate, w_one, w_two, w_three, g_own, g_other, *refs):
    stacks = refs[:9]
    grads = refs[9 : 9 + count]
    da_one_o, da_three_o, db_o, rate_grad, g = refs[9 + count :]
    step = pl.program_id(0)

    @pl.when(step == 0)
    def _():
        join_halves(idx, g_own, g_other, g)

    k, v, hidden, d_one, d_three, f_one, f_two, f_three, f_four = [ref[0] for ref in stacks]
    rows = k.shape[0]
    r = piece_rate(idx, rate, step + base, rows)
    v = v.astype(f32)
    t = (-r * v).astype(bf16)
    dd_one = dot_nn(k, g[0])
    dd_three = dot_nn(k, g[2])
    dh = dot_nt(t, g[1])
    f_one = f_one.astype(f32)
    f_two = f_two.astype(f32)
    f_three = f_three.astype(f32)
    f_four = f_four.astype(f32)
    db = (dd_one * f_one + dd_three * f_two).astype(bf16)
    da_three = (dd_one * f_three + dh * f_two).astype(bf16)
    da_one = (dd_one * f_four + dd_three * f_three + dh * f_one).astype(bf16)
    da_one_o[0] = da_one
    da_three_o[0] = da_three
    db_o[0] = db
    dt = dot_nn(hidden, g[1]) + dot_nn(db, w_two[...])
    gk = (
        (dot_nt(d_one, g[0]) + dot_nt(d_three, g[2]))
        + (dot_nt(da_one, w_one[...]) + dot_nt(da_three, w_three[...]))
    ).astype(bf16)
    gv = (-r * dt).astype(bf16)
    rate_grad[0] = -jnp.sum(v * dt, axis=1, keepdims=True)
    for i in range(count):

        @pl.when(step == i)
        def _():
            grads[i][0] = gk
            grads[i][1] = gv


def weights_kernel(count, idx, rate, keys, values, *refs):
    low, high = refs[:4], refs[4:8]
    keep, send, rate_out, kb, tb, a_one_b, a_three_b, bb = refs[8:]
    rows = keys.shape[1]
    split = low[0].shape[0]
    for p in range(count):
        at = slice(p * rows, (p + 1) * rows)
        source, s = (low, p) if p < split else (high, p - split)
        kb[at] = keys[p]
        tb[at] = (-piece_rate(idx, rate, p, rows) * values[p].astype(f32)).astype(bf16)
        a_one_b[at] = source[0][s]
        a_three_b[at] = source[1][s]
        bb[at] = source[2][s]
        rate_out[pl.ds(pl.multiple_of((idx[0] ^ p) * rows, rows), rows), :] = source[3][s]
    emit_halves(idx, ((kb, a_one_b), (bb, tb), (kb, a_three_b)), keep, send)


def join_kernel(idx, own_ref, other_ref, *outs):
    half = own_ref.shape[2]
    own, other = columns(idx, half)
    for j in range(3):
        outs[j][:, pl.ds(own, half)] = own_ref[j]
        outs[j][:, pl.ds(other, half)] = other_ref[j]


def call(kernel, operands, outs, scratch=()):
    smem = pl.BlockSpec(memory_space=pltpu.SMEM)
    vmem = pl.BlockSpec(memory_space=pltpu.VMEM)
    return pl.pallas_call(
        kernel,
        out_shape=outs,
        in_specs=[smem] + [vmem] * (len(operands) - 1),
        out_specs=[vmem] * len(outs),
        scratch_shapes=scratch,
    )(*operands)


def call_each(kernel, operands, outs):
    def spec(x):
        return pl.BlockSpec((1,) + x.shape[1:], lambda j: (j, 0, 0))

    return pl.pallas_call(
        kernel,
        grid=(3,),
        out_shape=outs,
        in_specs=[spec(x) for x in operands],
        out_specs=[spec(x) for x in outs],
    )(*operands)


def shape(dims, dtype):
    return jax.ShapeDtypeStruct(tuple(dims), dtype)


def xor_permute(x, axis, bit):
    size = lax.axis_size(axis)
    return lax.ppermute(x, axis, [(i, i ^ bit) for i in range(size)])


def body(queries, keys, values, rates, fast_one, fast_two, fast_three, grad_out):
    count = lax.axis_size("head")
    tok = lax.axis_size("tok")
    rows = keys.shape[1]
    fan_in, hidden_units = fast_one.shape[1], fast_one.shape[2]
    width = fan_in
    half = hidden_units // 2
    early = count // 2
    late = count - early
    head = lax.axis_index("head").astype(jnp.int32)
    core = lax.axis_index("tok").astype(jnp.int32) & 1
    idx = jnp.stack([head, core])
    weights = (fast_one[0], fast_two[0], fast_three[0])
    low = tuple(w.astype(bf16) for w in weights)
    weight_half = jnp.stack(
        [lax.dynamic_slice(w, (0, core * half), (fan_in, half)) for w in weights]
    )
    rate = rates.reshape(-1, 1)

    def exchange(pieces, first=1):
        return [
            piece if p == 0 else xor_permute(piece, "head", p)
            for p, piece in enumerate(pieces, first)
        ]

    def paste(pieces):
        out = jnp.zeros((rows, count * width), bf16)
        for p in reversed(range(count)):
            out = lax.dynamic_update_slice(out, pieces[p], (0, (head ^ p) * width))
        return out[None]

    def tok_exchange(keep, sent):
        mine = (keep + sent.astype(f32)).astype(bf16)
        bit = 2
        theirs = xor_permute(mine, "tok", bit)
        while bit * 2 < tok:
            bit *= 2
            mine = (mine.astype(f32) + theirs.astype(f32)).astype(bf16)
            theirs = xor_permute(mine, "tok", bit)
        return mine, theirs

    block = (3, fan_in, half)
    halves = [shape(block, f32), shape(block, bf16)]
    square = (3, fan_in, hidden_units)
    tokens = count * rows
    tall = (tokens, width)
    both = shape((2, rows, width), bf16)

    kv_cut = call(cut_kernel, (idx, keys[0], values[0]), [both] * count)
    qe_cut = call(cut_kernel, (idx, queries[0], grad_out[0]), [both] * count)
    kv = exchange(kv_cut, 0)
    qe = [qe_cut[0]]
    for p in range(1, count):
        kv[p], piece = lax.optimization_barrier((kv[p], qe_cut[p]))
        qe.append(xor_permute(piece, "head", p))

    keep, send = call(
        functools.partial(inner_kernel, count),
        (idx, rate, *low, *kv),
        halves,
        [pltpu.VMEM(tall, bf16)] * 5,
    )
    idx_late, send = lax.optimization_barrier((idx, send))
    mine, theirs = tok_exchange(keep, xor_permute(send, "tok", 1))
    stack = shape((count, rows, width), bf16)
    stacks = call(functools.partial(factor_kernel, count), (idx_late, rate, *low, *kv), [stack] * 9)
    update, stats, y_own = call_each(
        normalize_kernel,
        (mine, theirs, weight_half),
        [shape(block, f32), shape((3, 2, half), f32), shape(block, bf16)],
    )
    y_other = xor_permute(y_own, "tok", 1)
    begun = call(
        functools.partial(apply_early_kernel, early),
        (idx, y_own, y_other, *qe[:early]),
        [shape((early * rows, width), bf16)] * 5,
        [pltpu.VMEM(square, bf16)],
    )
    keep, send, d_one, d_three = call(
        functools.partial(apply_late_kernel, late),
        (idx, y_own, y_other, *qe[early:], *begun),
        halves + [shape(tall, bf16)] * 2,
        [pltpu.VMEM(tall, bf16)] * 3 + [pltpu.VMEM(square, bf16)],
    )
    mine, theirs = tok_exchange(keep, xor_permute(send, "tok", 1))
    grad_q = call(
        functools.partial(query_kernel, count),
        (idx, y_own, y_other, d_one, d_three),
        [shape((rows, width), bf16)] * count,
        [pltpu.VMEM(square, bf16)],
    )
    query_back = paste(exchange(grad_q, 0))
    cot_own, moment = call_each(
        adjoint_kernel,
        (mine, theirs, update, stats),
        [shape(block, bf16), shape((3, 1, half), f32)],
    )
    cot_other = xor_permute(cot_own, "tok", 1)

    def double(base, span):
        smem = pl.BlockSpec(memory_space=pltpu.SMEM)
        vmem = pl.BlockSpec(memory_space=pltpu.VMEM)
        read = pl.BlockSpec((1, rows, width), lambda p: (p + base, 0, 0))
        write = pl.BlockSpec((1, rows, width), lambda p: (p, 0, 0))
        column = pl.BlockSpec((1, rows, 1), lambda p: (p, 0, 0))
        res = pl.pallas_call(
            functools.partial(double_kernel, base, span),
            grid=(span,),
            out_shape=[both] * span
            + [shape((span, rows, width), bf16)] * 3
            + [shape((span, rows, 1), f32)],
            in_specs=[smem] + [vmem] * 6 + [read] * 9,
            out_specs=[vmem] * span + [write] * 3 + [column],
            scratch_shapes=[pltpu.VMEM(square, bf16)],
        )(idx, rate, *low, cot_own, cot_other, *stacks)
        return list(res[:span]), res[span:]

    grads_high, rest_high = double(early, late)
    grads_low, rest_low = double(0, early)
    kv_back = exchange(grads_low, 0) + exchange(grads_high, early)
    key_back = paste([piece[0] for piece in kv_back])
    value_back = paste([piece[1] for piece in kv_back])

    keep, send, rate_grad = call(
        functools.partial(weights_kernel, count),
        (idx, rate, *stacks[:2], *rest_low, *rest_high),
        halves + [shape((tokens, 1), f32)],
        [pltpu.VMEM(tall, bf16)] * 5,
    )
    ref_norm, upd_norm = stats[:, 0:1], stats[:, 1:2]
    factor = ref_norm / upd_norm
    direct = weight_half * (moment / (upd_norm * ref_norm)) + (
        factor * (mine.astype(f32) + theirs.astype(f32))
        - update * (factor * moment / (upd_norm * upd_norm))
    )
    chip = (keep + direct * (2.0 / tok)) + xor_permute(send, "tok", 1).astype(f32)
    stages = [("tok", 1 << b) for b in range(1, tok.bit_length() - 1)]
    stages_seq = [("seq", 1 << b) for b in range(lax.axis_size("seq").bit_length() - 1)]
    cut_row = fan_in // 2
    parts = []
    for part, order in (
        (chip[:, :cut_row], stages + stages_seq),
        (chip[:, cut_row:], stages_seq + stages),
    ):
        for axis, bit in order:
            part = part.astype(bf16)
            moved = xor_permute(part, axis, bit)
            part = part.astype(f32) + moved.astype(f32)
        parts.append(part)
    total_own = jnp.concatenate(parts, axis=1)
    total_other = xor_permute(total_own, "tok", 1)
    totals = call(
        join_kernel, (idx, total_own, total_other), [shape((fan_in, hidden_units), f32)] * 3
    )
    rate_grads = rate_grad.reshape(rates.shape)
    return (query_back, key_back, value_back, rate_grads, *(t[None] for t in totals))


def solution(mesh):
    tokens = P("seq", ("tok", "head"), None)
    placed = (
        tokens,
        tokens,
        tokens,
        P("seq", "head", "tok"),
        P("head", None, None),
        P("head", None, None),
        P("head", None, None),
        tokens,
    )
    return jax.shard_map(
        body,
        mesh=mesh,
        in_specs=placed,
        out_specs=(
            tokens,
            tokens,
            tokens,
            P("seq", "head", "tok"),
            P("head", None, None),
            P("head", None, None),
            P("head", None, None),
        ),
        check_vma=False,
    )
```

profile of v0, /device:TPU:0, one launch (start us, length us, event | category | flops | bytes accessed | tf_op | source)
XLA Modules:
  0.0 296.6 jit_solution(10455662968234550334)
XLA Ops:
  1.3 3.0 %shard_map.135 = (bf16[2,256,512]{2,1,0:T(8,128)(2,1)}, bf16[2,256,512]{2,1,0:T(8,128)(2,1)}, bf16[2,256,512]{2,1,0:T(8,128)(2,1)}, bf16[2,256,512]{2,1,0:T(8,128)(2,1)}) custom-call(s32[2]{0:T(128)} %pad_add_fusion.idx, bf16[256,2048]{1,0:T(8,128)(2,1)} %bitcast.34, bf16[256,2048]{1,0:T(8,128)(2,1)} %bitcast.35), custom_call_target="tpu_custom_call" | custom-call | tf_op jit(solution)/shard_map/pallas_call | solution.py:254
  4.3 3.1 %collective-permute-start = (bf16[2,256,512]{2,1,0:T(8,128)(2,1)}, bf16[2,256,512]{2,1,0:T(8,128)(2,1)S(1)}, u32[]{:S(2)}, u32[]{:S(2)}) collective-permute-start(bf16[2,256,512]{2,1,0:T(8,128)(2,1)} %get-tuple-element.71), channel_id=1, source_target_pairs={{0,2},{2,0},{4,6},{6,4},{1,3},{3,1},{5,7},{7,5},{8,10},{10,8},{12,... | collective-permute-start | bytes 1572872 | tf_op jit(solution)/shard_map/ppermute | solution.py:282
  7.3 2.6 collective-permute-start.1
  9.9 1.0 copy.15.rate
  11.0 3.2 %shard_map.136 = (bf16[2,256,512]{2,1,0:T(8,128)(2,1)}, bf16[2,256,512]{2,1,0:T(8,128)(2,1)}, bf16[2,256,512]{2,1,0:T(8,128)(2,1)}, bf16[2,256,512]{2,1,0:T(8,128)(2,1)}) custom-call(s32[2]{0:T(128)} %pad_add_fusion.idx, bf16[256,2048]{1,0:T(8,128)(2,1)} %bitcast.36, bf16[256,2048]{1,0:T(8,128)(2,1)} %bitcast.37), custom_call_target="tpu_custom_call" | custom-call | tf_op jit(solution)/shard_map/pallas_call | solution.py:254
  14.2 2.1 convert_bitcast_fusion.2.w_one
  16.3 1.1 convert_bitcast_fusion
  17.4 12.6 %collective-permute-done.refs_1_ = bf16[2,256,512]{2,1,0:T(8,128)(2,1)S(1)} collective-permute-done((bf16[2,256,512]{2,1,0:T(8,128)(2,1)}, bf16[2,256,512]{2,1,0:T(8,128)(2,1)S(1)}, u32[]{:S(2)}, u32[]{:S(2)}) %collective-permute-start) | collective-permute-done | bytes 524320 | tf_op jit(solution)/shard_map/ppermute | solution.py:282
  30.0 15.7 %collective-permute-done.1.refs_2_ = bf16[2,256,512]{2,1,0:T(8,128)(2,1)S(1)} collective-permute-done((bf16[2,256,512]{2,1,0:T(8,128)(2,1)}, bf16[2,256,512]{2,1,0:T(8,128)(2,1)S(1)}, u32[]{:S(2)}, u32[]{:S(2)}) %collective-permute-start.1) | collective-permute-done | bytes 524320 | tf_op jit(solution)/shard_map/ppermute | solution.py:282
  45.7 0.8 copy-done.14
  46.5 7.6 %shard_map.137 = (f32[3,512,256]{2,1,0:T(8,128)}, bf16[3,512,256]{2,1,0:T(8,128)(2,1)}) custom-call(s32[2]{0:T(128)} %pad_add_fusion.idx, f32[1024,1]{1,0:T(8,128)} %copy.15.rate, bf16[512,512]{1,0:T(8,128)(2,1)} %convert_bitcast_fusion.2.w_one, bf16[512,512]{1,0:T(8,128)(2,1)} %get-tuple-element.147.w_two, bf16[512,512]{1,0:T(8,128)(2,1)} %get-tuple-element.146.w_three, ...), custom_call_target="tpu_custom_call" | custom-call | tf_op jit(solution)/shard_map/pallas_call | solution.py:254
  54.1 2.5 collective-permute-done.3
  56.6 1.6 add_convert_fusion.2.mine
  58.3 1.6 collective-permute-start.4
  59.8 1.1 constant_dynamic-slice_fusion.2
  61.1 1.4 pad_maximum_fusion.weight
  62.6 15.5 %collective-permute-done.4.theirs = bf16[3,512,256]{2,1,0:T(8,128)(2,1)} collective-permute-done((bf16[3,512,256]{2,1,0:T(8,128)(2,1)S(1)}, bf16[3,512,256]{2,1,0:T(8,128)(2,1)}, u32[]{:S(2)}, u32[]{:S(2)}) %collective-permute-start.4) | collective-permute-done | bytes 786464 | tf_op jit(solution)/shard_map/ppermute | solution.py:282
  78.0 4.2 %shard_map.138 = (f32[3,512,256]{2,1,0:T(8,128)}, f32[3,2,256]{2,1,0:T(2,128)}, bf16[3,512,256]{2,1,0:T(8,128)(2,1)}) custom-call(bf16[3,512,256]{2,1,0:T(8,128)(2,1)} %copy-done.10, bf16[3,512,256]{2,1,0:T(8,128)(2,1)} %collective-permute-done.4.theirs, f32[3,512,256]{2,1,0:T(8,128)} %pad_maximum_fusion.weight), custom_call_target="tpu_custom_call" | custom-call | tf_op jit(solution)/shard_map/pallas_call | solution.py:267
  82.3 9.8 %collective-permute-start.8 = (bf16[2,256,512]{2,1,0:T(8,128)(2,1)}, bf16[2,256,512]{2,1,0:T(8,128)(2,1)S(1)}, u32[]{:S(2)}, u32[]{:S(2)}) collective-permute-start(bf16[2,256,512]{2,1,0:T(8,128)(2,1)} %get-tuple-element.87), channel_id=1, source_target_pairs={{0,2},{2,0},{4,6},{6,4},{1,3},{3,1},{5,7},{7,5},{8,10},{10,8},{12,... | collective-permute-start | bytes 1572872 | tf_op jit(solution)/shard_map/ppermute | solution.py:282
  92.0 1.1 collective-permute-start.6
  93.1 1.4 collective-permute-start.7
  94.6 21.1 %collective-permute-done.8.refs_1_ = bf16[2,256,512]{2,1,0:T(8,128)(2,1)S(1)} collective-permute-done((bf16[2,256,512]{2,1,0:T(8,128)(2,1)}, bf16[2,256,512]{2,1,0:T(8,128)(2,1)S(1)}, u32[]{:S(2)}, u32[]{:S(2)}) %collective-permute-start.8) | collective-permute-done | bytes 524320 | tf_op jit(solution)/shard_map/ppermute | solution.py:282
  115.7 0.8 copy-done.17
  116.9 4.2 %shard_map.139 = (bf16[512,512]{1,0:T(8,128)(2,1)}, bf16[512,512]{1,0:T(8,128)(2,1)}, bf16[512,512]{1,0:T(8,128)(2,1)}, bf16[512,512]{1,0:T(8,128)(2,1)}, bf16[512,512]{1,0:T(8,128)(2,1)}) custom-call(s32[2]{0:T(128)} %pad_add_fusion.idx, bf16[3,512,256]{2,1,0:T(8,128)(2,1)} %get-tuple-element.83.y_own, bf16[3,512,256]{2,1,0:T(8,128)(2,1)} %copy-done.2, ...), custom_call_target="tpu_custom_call" | custom-call | tf_op jit(solution)/shard_map/pallas_call | solution.py:254
  121.1 9.2 %collective-permute-done.6.refs_0_ = bf16[2,256,512]{2,1,0:T(8,128)(2,1)S(1)} collective-permute-done((bf16[2,256,512]{2,1,0:T(8,128)(2,1)S(1)}, bf16[2,256,512]{2,1,0:T(8,128)(2,1)S(1)}, u32[]{:S(2)}, u32[]{:S(2)}) %collective-permute-start.6) | collective-permute-done | bytes 524320 | tf_op jit(solution)/shard_map/ppermute | solution.py:282
  130.3 0.8 copy-done.18
  131.2 6.9 %shard_map.140 = (f32[3,512,256]{2,1,0:T(8,128)}, bf16[3,512,256]{2,1,0:T(8,128)(2,1)}, bf16[1024,512]{1,0:T(8,128)(2,1)}, bf16[1024,512]{1,0:T(8,128)(2,1)}) custom-call(s32[2]{0:T(128)} %pad_add_fusion.idx, bf16[3,512,256]{2,1,0:T(8,128)(2,1)} %get-tuple-element.83.y_own, bf16[3,512,256]{2,1,0:T(8,128)(2,1)} %copy-done.2, bf16[2,256,512]{2,1,0:T(8,128)(2,1)} %copy-done.18, ...), custom_call_target="tpu_custom_call" | custom-call | tf_op jit(solution)/shard_map/pallas_call | solution.py:254
  138.1 2.5 collective-permute-done.12
  140.6 1.6 add_convert_fusion.1.mine
  142.2 1.6 collective-permute-start.13
  143.8 18.1 %collective-permute-done.13.theirs = bf16[3,512,256]{2,1,0:T(8,128)(2,1)S(1)} collective-permute-done((bf16[3,512,256]{2,1,0:T(8,128)(2,1)S(1)}, bf16[3,512,256]{2,1,0:T(8,128)(2,1)S(1)}, u32[]{:S(2)}, u32[]{:S(2)}) %collective-permute-start.13) | collective-permute-done | bytes 786464 | tf_op jit(solution)/shard_map/ppermute | solution.py:282
  161.9 0.9 copy-done.9
  162.7 3.7 %shard_map.142 = (bf16[3,512,256]{2,1,0:T(8,128)(2,1)}, f32[3,1,256]{2,1,0:T(1,128)}) custom-call(bf16[3,512,256]{2,1,0:T(8,128)(2,1)} %copy-done, bf16[3,512,256]{2,1,0:T(8,128)(2,1)} %copy-done.9, f32[3,512,256]{2,1,0:T(8,128)} %get-tuple-element.101.update, f32[3,2,256]{2,1,0:T(2,128)} %get-tuple-element.102.stats), custom_call_target="tpu_custom_call" | custom-call | tf_op jit(solution)/shard_map/pallas_call | solution.py:267
  166.5 8.3 %shard_map.143 = (bf16[4,256,512]{2,1,0:T(8,128)(2,1)}, bf16[4,256,512]{2,1,0:T(8,128)(2,1)}, bf16[4,256,512]{2,1,0:T(8,128)(2,1)}, bf16[4,256,512]{2,1,0:T(8,12...) custom-call(s32[2]{0:T(128)} %pad_add_fusion.idx, ...), custom_call_target="tpu_custom_call" | custom-call | tf_op jit(solution)/shard_map/pallas_call | solution.py:254
  174.7 0.9 copy-done.8
  175.6 8.1 %shard_map.144 = (bf16[2,256,512]{2,1,0:T(8,128)(2,1)}, bf16[2,256,512]{2,1,0:T(8,128)(2,1)}, bf16[2,256,512]{2,1,0:T(8,128)(2,1)}, bf16[2,256,512]{2,1,0:T(8,12...) custom-call(s32[2]{0:T(128)} %pad_add_fusion.idx, f32[1024,1]{1,0:T(8,128)} %copy.15.rate, ...), custom_call_target="tpu_custom_call" | custom-call | tf_op jit(solution)/shard_map/pallas_call | solution.py:390
  183.7 8.0 %shard_map.145 = (bf16[2,256,512]{2,1,0:T(8,128)(2,1)}, bf16[2,256,512]{2,1,0:T(8,128)(2,1)}, bf16[2,256,512]{2,1,0:T(8,128)(2,1)}, bf16[2,256,512]{2,1,0:T(8,12...) custom-call(s32[2]{0:T(128)} %pad_add_fusion.idx, f32[1024,1]{1,0:T(8,128)} %copy.15.rate, ...), custom_call_target="tpu_custom_call" | custom-call | tf_op jit(solution)/shard_map/pallas_call | solution.py:390
  191.8 6.3 %shard_map.146 = (f32[3,512,256]{2,1,0:T(8,128)}, bf16[3,512,256]{2,1,0:T(8,128)(2,1)}, f32[1024,1]{1,0:T(8,128)}) custom-call(s32[2]{0:T(128)} %pad_add_fusion.idx, f32[1024,1]{1,0:T(8,128)} %copy.15.rate, bf16[4,256,512]{2,1,0:T(8,128)(2,1)} %get-tuple-element.105.refs_0_.keys, bf16[4,256,512]{2,1,0:T(8,128)(2,1)} %get-tuple-element.106.refs_1_.values, ...), custom_call_target="tpu_custom_call" | custom-call | tf_op jit(solution)/shard_map/pallas_call | solution.py:254
  198.6 2.1 collective-permute-done.18
  200.7 2.7 add_convert_fusion
  203.5 1.6 collective-permute-start.19
  205.1 1.5 collective-permute-start.21
  206.6 4.1 %shard_map.141 = (bf16[256,512]{1,0:T(8,128)(2,1)}, bf16[256,512]{1,0:T(8,128)(2,1)}, bf16[256,512]{1,0:T(8,128)(2,1)}, bf16[256,512]{1,0:T(8,128)(2,1)}) custom-call(s32[2]{0:T(128)} %pad_add_fusion.idx, bf16[3,512,256]{2,1,0:T(8,128)(2,1)} %get-tuple-element.83.y_own, bf16[3,512,256]{2,1,0:T(8,128)(2,1)} %copy-done.2, ...), custom_call_target="tpu_custom_call" | custom-call | tf_op jit(solution)/shard_map/pallas_call | solution.py:254
  210.7 2.5 collective-permute-start.9
  213.2 9.9 %collective-permute-start.10 = (bf16[256,512]{1,0:T(8,128)(2,1)}, bf16[256,512]{1,0:T(8,128)(2,1)S(1)}, u32[]{:S(2)}, u32[]{:S(2)}) collective-permute-start(bf16[256,512]{1,0:T(8,128)(2,1)} %get-tuple-element.96), channel_id=1, source_target_pairs={{0,4},{2,6},{4,0},{6,2},{1,5},{3,7},{5,1},{7,3},{8,12},{10,14},{12... | collective-permute-start | bytes 786440 | tf_op jit(solution)/shard_map/ppermute | solution.py:282
  224.0 1.1 broadcast_in_dim.22.clone
  226.3 14.2 %collective-permute-done.10 = bf16[256,512]{1,0:T(8,128)(2,1)S(1)} collective-permute-done((bf16[256,512]{1,0:T(8,128)(2,1)}, bf16[256,512]{1,0:T(8,128)(2,1)S(1)}, u32[]{:S(2)}, u32[]{:S(2)}) %collective-permute-start.10) | collective-permute-done | bytes 262176 | tf_op jit(solution)/shard_map/ppermute | solution.py:282
  240.5 0.7 bitcast_dynamic-update-slice_fusion.2
  241.2 2.5 collective-permute-start.15
  244.1 0.9 bitcast_dynamic-update-slice_fusion.1
  245.0 4.5 %collective-permute-start.16 = (bf16[2,256,512]{2,1,0:T(8,128)(2,1)}, bf16[2,256,512]{2,1,0:T(8,128)(2,1)}, u32[]{:S(2)}, u32[]{:S(2)}) collective-permute-start(bf16[2,256,512]{2,1,0:T(8,128)(2,1)} %get-tuple-element.115), channel_id=1, source_target_pairs={{0,4},{2,6},{4,0},{6,2},{1,5},{3,7},{5,1},{7,3},{8,12},{10,14},{12... | collective-permute-start | bytes 1572872 | tf_op jit(solution)/shard_map/ppermute | solution.py:282
  249.4 0.7 bitcast_dynamic-update-slice_fusion
  250.2 1.8 reduce
  252.0 6.2 %collective-permute-done.15 = bf16[2,256,512]{2,1,0:T(8,128)(2,1)} collective-permute-done((bf16[2,256,512]{2,1,0:T(8,128)(2,1)}, bf16[2,256,512]{2,1,0:T(8,128)(2,1)}, u32[]{:S(2)}, u32[]{:S(2)}) %collective-permute-start.15) | collective-permute-done | bytes 524320 | tf_op jit(solution)/shard_map/ppermute | solution.py:282
  258.2 1.1 broadcast_in_dim.22.clone.1
  259.3 1.7 slice_dynamic-update-slice_fusion.2
  260.9 1.1 broadcast_in_dim.22.clone.2
  262.0 1.7 slice_dynamic-update-slice_fusion.5
  263.8 23.5 %collective-permute-done.16 = bf16[2,256,512]{2,1,0:T(8,128)(2,1)} collective-permute-done((bf16[2,256,512]{2,1,0:T(8,128)(2,1)}, bf16[2,256,512]{2,1,0:T(8,128)(2,1)}, u32[]{:S(2)}, u32[]{:S(2)}) %collective-permute-start.16) | collective-permute-done | bytes 524320 | tf_op jit(solution)/shard_map/ppermute | solution.py:282
  287.2 1.9 slice_dynamic-update-slice_fusion.1
  289.1 1.9 slice_dynamic-update-slice_fusion
  291.0 0.8 slice_dynamic-update-slice_fusion.6
  291.8 1.1 copy-done.15
  292.9 3.7 %shard_map.147 = (f32[512,512]{1,0:T(8,128)}, f32[512,512]{1,0:T(8,128)}, f32[512,512]{1,0:T(8,128)}) custom-call(s32[2]{0:T(128)} %pad_add_fusion.idx, f32[3,512,256]{2,1,0:T(8,128)} %copy-done.3, f32[3,512,256]{2,1,0:T(8,128)} %copy-done.15), custom_call_target="tpu_custom_call" | custom-call | tf_op jit(solution)/shard_map/pallas_call | solution.py:254
  (81 shorter events, 4.6 us)
Async XLA Ops:
  0.6 9.3 %copy-start.22 = (f32[1,1,1024]{2,1,0:T(1,128)S(1)}, f32[1,1,1024]{2,1,0:T(1,128)}, u32[]{:S(2)}) copy-start(f32[1,1,1024]{2,1,0:T(1,128)} %param.11) | copy-start | bytes 12292
  4.3 25.7 %collective-permute-start = (bf16[2,256,512]{2,1,0:T(8,128)(2,1)}, bf16[2,256,512]{2,1,0:T(8,128)(2,1)S(1)}, u32[]{:S(2)}, u32[]{:S(2)}) collective-permute-start(bf16[2,256,512]{2,1,0:T(8,128)(2,1)} %get-tuple-element.71), channel_id=1, source_target_pairs={{0,2},{2,0},{4,6},{6,4},{1,3},{3,1},{5,7},{7,5},{8,10},{10,8},{12,... | collective-permute-start | bytes 1572872 | tf_op jit(solution)/shard_map/ppermute | solution.py:282
  7.3 38.4 %collective-permute-start.1 = (bf16[2,256,512]{2,1,0:T(8,128)(2,1)}, bf16[2,256,512]{2,1,0:T(8,128)(2,1)S(1)}, u32[]{:S(2)}, u32[]{:S(2)}) collective-permute-start(bf16[2,256,512]{2,1,0:T(8,128)(2,1)} %get-tuple-element.74), channel_id=1, source_target_pairs={{0,4},{2,6},{4,0},{6,2},{1,5},{3,7},{5,1},{7,3},{8,12},{10,14},{12... | collective-permute-start | bytes 1572872 | tf_op jit(solution)/shard_map/ppermute | solution.py:282
  9.9 35.8 %collective-permute-start.2 = (bf16[2,256,512]{2,1,0:T(8,128)(2,1)}, bf16[2,256,512]{2,1,0:T(8,128)(2,1)}, u32[]{:S(2)}, u32[]{:S(2)}) collective-permute-start(bf16[2,256,512]{2,1,0:T(8,128)(2,1)} %get-tuple-element.77), channel_id=1, source_target_pairs={{0,6},{2,4},{4,2},{6,0},{1,7},{3,5},{5,3},{7,1},{8,14},{10,12},{12... | collective-permute-start | bytes 1572872 | tf_op jit(solution)/shard_map/ppermute | solution.py:282
  11.0 5.3 %copy-start.11 = (f32[1,512,512]{2,1,0:T(8,128)S(1)}, f32[1,512,512]{2,1,0:T(8,128)}, u32[]{:S(2)}) copy-start(f32[1,512,512]{2,1,0:T(8,128)} %param.14) | copy-start | bytes 3145732
  11.0 5.3 %copy-start.12 = (f32[1,512,512]{2,1,0:T(8,128)S(1)}, f32[1,512,512]{2,1,0:T(8,128)}, u32[]{:S(2)}) copy-start(f32[1,512,512]{2,1,0:T(8,128)} %param.13) | copy-start | bytes 3145732
  30.0 15.8 %copy-start.13 = (bf16[2,256,512]{2,1,0:T(8,128)(2,1)}, bf16[2,256,512]{2,1,0:T(8,128)(2,1)S(1)}, u32[]{:S(2)}) copy-start(bf16[2,256,512]{2,1,0:T(8,128)(2,1)S(1)} %collective-permute-done.refs_1_) | copy-start | bytes 1572868
  45.7 0.8 copy-start.14
  54.1 2.5 collective-permute-start.3
  58.3 2.8 copy-start.10
  58.3 19.8 %collective-permute-start.4 = (bf16[3,512,256]{2,1,0:T(8,128)(2,1)S(1)}, bf16[3,512,256]{2,1,0:T(8,128)(2,1)}, u32[]{:S(2)}, u32[]{:S(2)}) collective-permute-start(bf16[3,512,256]{2,1,0:T(8,128)(2,1)S(1)} %add_convert_fusion.2.mine), channel_id=1, source_target_pairs={{0,16},{8,24},{16,0},{24,8},{1,17},{9,25},{17,1},{25,9},{2,18},{10... | collective-permute-start | bytes 2359304 | tf_op jit(solution)/shard_map/ppermute | solution.py:282
  60.9 1.5 copy-start.7
  61.1 1.4 copy-start.5
  61.1 1.5 copy-start.6
  62.6 29.5 %copy-start.25 = (bf16[2,256,512]{2,1,0:T(8,128)(2,1)S(1)}, bf16[2,256,512]{2,1,0:T(8,128)(2,1)}, u32[]{:S(2)}) copy-start(bf16[2,256,512]{2,1,0:T(8,128)(2,1)} %get-tuple-element.84) | copy-start | bytes 1572868
  62.6 30.6 %copy-start.24 = (bf16[2,256,512]{2,1,0:T(8,128)(2,1)S(1)}, bf16[2,256,512]{2,1,0:T(8,128)(2,1)}, u32[]{:S(2)}) copy-start(bf16[2,256,512]{2,1,0:T(8,128)(2,1)} %get-tuple-element.85) | copy-start | bytes 1572868
  82.3 33.5 %collective-permute-start.5 = (bf16[3,512,256]{2,1,0:T(8,128)(2,1)}, bf16[3,512,256]{2,1,0:T(8,128)(2,1)S(1)}, u32[]{:S(2)}, u32[]{:S(2)}) collective-permute-start(bf16[3,512,256]{2,1,0:T(8,128)(2,1)} %get-tuple-element.83.y_own), channel_id=1, source_target_pairs={{0,8},{8,0},{16,24},{24,16},{1,9},{9,1},{17,25},{25,17},{2,10},{10... | collective-permute-start | bytes 2359304 | tf_op jit(solution)/shard_map/ppermute | solution.py:282
  82.3 33.5 %collective-permute-start.8 = (bf16[2,256,512]{2,1,0:T(8,128)(2,1)}, bf16[2,256,512]{2,1,0:T(8,128)(2,1)S(1)}, u32[]{:S(2)}, u32[]{:S(2)}) collective-permute-start(bf16[2,256,512]{2,1,0:T(8,128)(2,1)} %get-tuple-element.87), channel_id=1, source_target_pairs={{0,2},{2,0},{4,6},{6,4},{1,3},{3,1},{5,7},{7,5},{8,10},{10,8},{12,... | collective-permute-start | bytes 1572872 | tf_op jit(solution)/shard_map/ppermute | solution.py:282
  92.0 38.2 %collective-permute-start.6 = (bf16[2,256,512]{2,1,0:T(8,128)(2,1)S(1)}, bf16[2,256,512]{2,1,0:T(8,128)(2,1)S(1)}, u32[]{:S(2)}, u32[]{:S(2)}) collective-permute-start(bf16[2,256,512]{2,1,0:T(8,128)(2,1)S(1)} %copy-done.25), channel_id=1, source_target_pairs={{0,4},{2,6},{4,0},{6,2},{1,5},{3,7},{5,1},{7,3},{8,12},{10,14},{12... | collective-permute-start | bytes 1572872 | tf_op jit(solution)/shard_map/ppermute | solution.py:282
  93.1 37.1 %collective-permute-start.7 = (bf16[2,256,512]{2,1,0:T(8,128)(2,1)S(1)}, bf16[2,256,512]{2,1,0:T(8,128)(2,1)S(1)}, u32[]{:S(2)}, u32[]{:S(2)}) collective-permute-start(bf16[2,256,512]{2,1,0:T(8,128)(2,1)S(1)} %copy-done.24), channel_id=1, source_target_pairs={{0,6},{2,4},{4,2},{6,0},{1,7},{3,5},{5,3},{7,1},{8,14},{10,12},{12... | collective-permute-start | bytes 1572872 | tf_op jit(solution)/shard_map/ppermute | solution.py:282
  115.7 0.8 copy-start.17
  115.7 1.1 copy-start.2
  130.2 0.8 copy-start.18
  130.3 1.0 copy-start.19
  138.1 2.5 collective-permute-start.12
  142.2 19.7 %copy-start = (bf16[3,512,256]{2,1,0:T(8,128)(2,1)}, bf16[3,512,256]{2,1,0:T(8,128)(2,1)S(1)}, u32[]{:S(2)}) copy-start(bf16[3,512,256]{2,1,0:T(8,128)(2,1)S(1)} %add_convert_fusion.1.mine) | copy-start | bytes 2359300
  142.2 19.6 %collective-permute-start.13 = (bf16[3,512,256]{2,1,0:T(8,128)(2,1)S(1)}, bf16[3,512,256]{2,1,0:T(8,128)(2,1)S(1)}, u32[]{:S(2)}, u32[]{:S(2)}) collective-permute-start(bf16[3,512,256]{2,1,0:T(8,128)(2,1)S(1)} %add_convert_fusion.1.mine), channel_id=1, source_target_pairs={{0,16},{8,24},{16,0},{24,8},{1,17},{9,25},{17,1},{25,9},{2,18},{10... | collective-permute-start | bytes 2359304 | tf_op jit(solution)/shard_map/ppermute | solution.py:282
  161.9 0.9 copy-start.9
  166.5 8.3 %collective-permute-start.14 = (bf16[3,512,256]{2,1,0:T(8,128)(2,1)}, bf16[3,512,256]{2,1,0:T(8,128)(2,1)S(1)}, u32[]{:S(2)}, u32[]{:S(2)}) collective-permute-start(bf16[3,512,256]{2,1,0:T(8,128)(2,1)} %get-tuple-element.103.g_own), channel_id=1, source_target_pairs={{0,8},{8,0},{16,24},{24,16},{1,9},{9,1},{17,25},{25,17},{2,10},{10... | collective-permute-start | bytes 2359304 | tf_op jit(solution)/shard_map/ppermute | solution.py:282
  174.7 0.9 copy-start.8
  191.7 6.8 %copy-start.21 = (f32[3,2,256]{2,1,0:T(2,128)S(1)}, f32[3,2,256]{2,1,0:T(2,128)}, u32[]{:S(2)}) copy-start(f32[3,2,256]{2,1,0:T(2,128)} %get-tuple-element.102.stats) | copy-start | bytes 18436
  191.8 6.8 %copy-start.23 = (f32[3,1,256]{2,1,0:T(1,128)S(1)}, f32[3,1,256]{2,1,0:T(1,128)}, u32[]{:S(2)}) copy-start(f32[3,1,256]{2,1,0:T(1,128)} %get-tuple-element.128) | copy-start | bytes 9220
  191.8 8.9 %copy-start.1 = (bf16[3,512,256]{2,1,0:T(8,128)(2,1)S(1)}, bf16[3,512,256]{2,1,0:T(8,128)(2,1)}, u32[]{:S(2)}) copy-start(bf16[3,512,256]{2,1,0:T(8,128)(2,1)} %copy-done) | copy-start | bytes 2359300
  191.8 8.9 %copy-start.4 = (f32[3,512,256]{2,1,0:T(8,128)S(1)}, f32[3,512,256]{2,1,0:T(8,128)}, u32[]{:S(2)}) copy-start(f32[3,512,256]{2,1,0:T(8,128)} %get-tuple-element.101.update) | copy-start | bytes 4718596
  198.1 2.6 collective-permute-start.18
  203.5 19.7 %collective-permute-start.19 = (bf16[3,256,256]{2,1,0:T(8,128)(2,1)S(1)}, bf16[3,256,256]{2,1,0:T(8,128)(2,1)S(1)}, u32[]{:S(2)}, u32[]{:S(2)}) collective-permute-start(bf16[3,256,256]{2,1,0:T(8,128)(2,1)S(1)} %get-tuple-element.137), channel_id=1, source_target_pairs={{0,16},{8,24},{16,0},{24,8},{1,17},{9,25},{17,1},{25,9},{2,18},{10... | collective-permute-start | bytes 1179656 | tf_op jit(solution)/shard_map/ppermute | solution.py:282
  205.1 18.1 %collective-permute-start.21 = (bf16[3,256,256]{2,1,0:T(8,128)(2,1)S(1)}, bf16[3,256,256]{2,1,0:T(8,128)(2,1)S(1)}, u32[]{:S(2)}, u32[]{:S(2)}) collective-permute-start(bf16[3,256,256]{2,1,0:T(8,128)(2,1)S(1)} %get-tuple-element.138), channel_id=1, source_target_pairs={{0,1},{1,0},{2,3},{3,2},{4,5},{5,4},{6,7},{7,6},{8,9},{9,8},{10,11... | collective-permute-start | bytes 1179656 | tf_op jit(solution)/shard_map/ppermute | solution.py:282
  210.7 13.3 %collective-permute-start.9 = (bf16[256,512]{1,0:T(8,128)(2,1)}, bf16[256,512]{1,0:T(8,128)(2,1)S(1)}, u32[]{:S(2)}, u32[]{:S(2)}) collective-permute-start(bf16[256,512]{1,0:T(8,128)(2,1)} %get-tuple-element.95), channel_id=1, source_target_pairs={{0,6},{2,4},{4,2},{6,0},{1,7},{3,5},{5,3},{7,1},{8,14},{10,12},{12... | collective-permute-start | bytes 786440 | tf_op jit(solution)/shard_map/ppermute | solution.py:282
  213.2 27.3 %collective-permute-start.10 = (bf16[256,512]{1,0:T(8,128)(2,1)}, bf16[256,512]{1,0:T(8,128)(2,1)S(1)}, u32[]{:S(2)}, u32[]{:S(2)}) collective-permute-start(bf16[256,512]{1,0:T(8,128)(2,1)} %get-tuple-element.96), channel_id=1, source_target_pairs={{0,4},{2,6},{4,0},{6,2},{1,5},{3,7},{5,1},{7,3},{8,12},{10,14},{12... | collective-permute-start | bytes 786440 | tf_op jit(solution)/shard_map/ppermute | solution.py:282
  223.1 21.1 %collective-permute-start.11 = (bf16[256,512]{1,0:T(8,128)(2,1)}, bf16[256,512]{1,0:T(8,128)(2,1)S(1)}, u32[]{:S(2)}, u32[]{:S(2)}) collective-permute-start(bf16[256,512]{1,0:T(8,128)(2,1)} %get-tuple-element.97), channel_id=1, source_target_pairs={{0,2},{2,0},{4,6},{6,4},{1,3},{3,1},{5,7},{7,5},{8,10},{10,8},{12,... | collective-permute-start | bytes 786440 | tf_op jit(solution)/shard_map/ppermute | solution.py:282
  223.4 20.3 %collective-permute-start.22 = (bf16[3,256,256]{2,1,0:T(8,128)(2,1)S(1)}, bf16[3,256,256]{2,1,0:T(8,128)(2,1)S(1)}, u32[]{:S(2)}, u32[]{:S(2)}) collective-permute-start(bf16[3,256,256]{2,1,0:T(8,128)(2,1)S(1)} %get-tuple-element.136), channel_id=1, source_target_pairs={{0,16},{8,24},{16,0},{24,8},{1,17},{9,25},{17,1},{25,9},{2,18},{10... | collective-permute-start | bytes 1179656 | tf_op jit(solution)/shard_map/ppermute | solution.py:282
  225.8 18.0 %collective-permute-start.20 = (bf16[3,256,256]{2,1,0:T(8,128)(2,1)S(1)}, bf16[3,256,256]{2,1,0:T(8,128)(2,1)S(1)}, u32[]{:S(2)}, u32[]{:S(2)}) collective-permute-start(bf16[3,256,256]{2,1,0:T(8,128)(2,1)S(1)} %get-tuple-element.135), channel_id=1, source_target_pairs={{0,1},{1,0},{2,3},{3,2},{4,5},{5,4},{6,7},{7,6},{8,9},{9,8},{10,11... | collective-permute-start | bytes 1179656 | tf_op jit(solution)/shard_map/ppermute | solution.py:282
  241.2 17.0 %collective-permute-start.15 = (bf16[2,256,512]{2,1,0:T(8,128)(2,1)}, bf16[2,256,512]{2,1,0:T(8,128)(2,1)}, u32[]{:S(2)}, u32[]{:S(2)}) collective-permute-start(bf16[2,256,512]{2,1,0:T(8,128)(2,1)} %get-tuple-element.114), channel_id=1, source_target_pairs={{0,6},{2,4},{4,2},{6,0},{1,7},{3,5},{5,3},{7,1},{8,14},{10,12},{12... | collective-permute-start | bytes 1572872 | tf_op jit(solution)/shard_map/ppermute | solution.py:282
  243.9 5.5 %copy-start.20 = (bf16[256,512]{1,0:T(8,128)(2,1)S(1)}, bf16[256,512]{1,0:T(8,128)(2,1)}, u32[]{:S(2)}) copy-start(bf16[256,512]{1,0:T(8,128)(2,1)} %get-tuple-element.98) | copy-start | bytes 786436
  244.0 16.9 %copy-start.3 = (f32[3,512,256]{2,1,0:T(8,128)}, f32[3,512,256]{2,1,0:T(8,128)S(1)}, u32[]{:S(2)}) copy-start(f32[3,512,256]{2,1,0:T(8,128)S(1)} %pad_maximum_fusion.1.own_ref) | copy-start | bytes 4718596
  244.0 47.7 %collective-permute-start.23 = (f32[3,512,256]{2,1,0:T(8,128)S(1)}, f32[3,512,256]{2,1,0:T(8,128)S(1)}, u32[]{:S(2)}, u32[]{:S(2)}) collective-permute-start(f32[3,512,256]{2,1,0:T(8,128)S(1)} %pad_maximum_fusion.1.own_ref), channel_id=1, source_target_pairs={{0,8},{8,0},{16,24},{24,16},{1,9},{9,1},{17,25},{25,17},{2,10},{10... | collective-permute-start | bytes 4718600 | tf_op jit(solution)/shard_map/ppermute | solution.py:282
  245.0 42.3 %collective-permute-start.16 = (bf16[2,256,512]{2,1,0:T(8,128)(2,1)}, bf16[2,256,512]{2,1,0:T(8,128)(2,1)}, u32[]{:S(2)}, u32[]{:S(2)}) collective-permute-start(bf16[2,256,512]{2,1,0:T(8,128)(2,1)} %get-tuple-element.115), channel_id=1, source_target_pairs={{0,4},{2,6},{4,0},{6,2},{1,5},{3,7},{5,1},{7,3},{8,12},{10,14},{12... | collective-permute-start | bytes 1572872 | tf_op jit(solution)/shard_map/ppermute | solution.py:282
  250.2 38.9 %collective-permute-start.17 = (bf16[2,256,512]{2,1,0:T(8,128)(2,1)}, bf16[2,256,512]{2,1,0:T(8,128)(2,1)}, u32[]{:S(2)}, u32[]{:S(2)}) collective-permute-start(bf16[2,256,512]{2,1,0:T(8,128)(2,1)} %get-tuple-element.116), channel_id=1, source_target_pairs={{0,2},{2,0},{4,6},{6,4},{1,3},{3,1},{5,7},{7,5},{8,10},{10,8},{12,... | collective-permute-start | bytes 1572872 | tf_op jit(solution)/shard_map/ppermute | solution.py:282
  262.0 28.9 %copy-start.16 = (bf16[2,256,512]{2,1,0:T(8,128)(2,1)S(1)}, bf16[2,256,512]{2,1,0:T(8,128)(2,1)}, u32[]{:S(2)}) copy-start(bf16[2,256,512]{2,1,0:T(8,128)(2,1)} %get-tuple-element.117) | copy-start | bytes 1572868
  291.8 1.1 copy-start.15
where the time goes:
time: 297 us
  waiting for transfers between devices  143 us (48%)
  Pallas kernels  71.3 us (24%)
  starting transfers between devices  45.2 us (15%)
  local copies, waits for them, and re-layouts  22.5 us (8%)
  other arithmetic  13.5 us (5%)
    ppermute x24, waiting for transfers between devices, xor_permute(): return lax.ppermute(x, axis, [(i, i ^ bit) for i in range(size)])  143 us
    pallas_call x9, Pallas kernels, call(): pl.pallas_call(kernel, out_shape=outs, in_specs=[smem] + [vmem] * (len(op...  47.3 us
    ppermute x24, starting transfers between devices, xor_permute(): return lax.ppermute(x, axis, [(i, i ^ bit) for i in range(size)])  45.2 us
    pallas_call x2, Pallas kernels, double(): pl.pallas_call(functools.partial(double_kernel, base, span), grid=(span,)...  16.1 us
    dynamic_update_slice x9, local copies, waits for them, and re-layouts, paste(): out = lax.dynamic_update_slice(out, pieces[p], (0, (head ^ p) * width))  10.9 us
    pallas_call x2, Pallas kernels, call_each(): pl.pallas_call(kernel, grid=(3,), out_shape=outs, in_specs=[spec(x) for x...  7.94 us
    unnamed x55, local copies, waits for them, and re-layouts  5.99 us
  transfers between devices with their start and end apart: 24, of which 12 were waited for; matrix products, arithmetic and copies ran while one was open for 8% of the time, Pallas kernels for 7%

commit v1 on v0

v1 whole, which is shorter than its diff:
```python
import functools

import jax
import jax.numpy as jnp
from jax import lax
from jax.experimental import pallas as pl
from jax.experimental.pallas import tpu as pltpu
from jax.sharding import PartitionSpec as P


epsilon = 1e-06
bf16 = jnp.bfloat16
f32 = jnp.float32


def dot_nn(left, right):
    return lax.dot_general(left, right, (((1,), (0,)), ((), ())), preferred_element_type=f32)


def dot_nt(left, right):
    return lax.dot_general(left, right, (((1,), (1,)), ((), ())), preferred_element_type=f32)


def sigmoid(x):
    return 0.5 * jnp.tanh(0.5 * x) + 0.5


def columns(idx, half):
    own = pl.multiple_of(idx[1] * half, half)
    other = pl.multiple_of((1 - idx[1]) * half, half)
    return own, other


def emit_halves(idx, pairs, keep, send, extra=None):
    half = keep.shape[2]
    own, other = columns(idx, half)
    for j, (left, right) in enumerate(pairs):
        send[j] = dot_nn(left[...], right[:, pl.ds(other, half)]).astype(bf16)
    for j, (left, right) in enumerate(pairs):
        total = dot_nn(left[...], right[:, pl.ds(own, half)])
        keep[j] = total if extra is None else total + extra(j)


def join_halves(idx, own_ref, other_ref, out):
    half = own_ref.shape[2]
    own, other = columns(idx, half)
    for j in range(3):
        out[j, :, pl.ds(own, half)] = own_ref[j]
        out[j, :, pl.ds(other, half)] = other_ref[j]


def piece_rate(idx, rate, piece, rows):
    return rate[pl.ds(pl.multiple_of((idx[0] ^ piece) * rows, rows), rows), :]


def cut_kernel(idx, left, right, *outs):
    width = outs[0].shape[2]
    for p, out in enumerate(outs):
        lanes = pl.ds(pl.multiple_of((idx[0] ^ p) * width, width), width)
        out[0] = left[:, lanes]
        out[1] = right[:, lanes]


def inner_kernel(count, idx, rate, w_one, w_two, w_three, *refs):
    pieces = refs[:count]
    keep, send, kt, tb, ht, d_one_b, d_three_b = refs[count:]
    rows = pieces[0].shape[1]
    for p in range(count):
        at = slice(p * rows, (p + 1) * rows)
        k = pieces[p][0]
        t = (-piece_rate(idx, rate, p, rows) * pieces[p][1].astype(f32)).astype(bf16)
        a_one = dot_nn(k, w_one[...])
        a_three = dot_nn(k, w_three[...])
        b = dot_nt(t, w_two[...])
        sq = sigmoid(a_one)
        swished = a_one * sq
        slope = sq * (1.0 + a_one * (1.0 - sq))
        kt[:, at] = k.T
        tb[at] = t
        ht[:, at] = (swished * a_three).astype(bf16).T
        d_one_b[at] = (b * a_three * slope).astype(bf16)
        d_three_b[at] = (b * swished).astype(bf16)
    emit_halves(idx, ((kt, d_one_b), (ht, tb), (kt, d_three_b)), keep, send)


def factor_kernel(count, idx, rate, w_one, w_two, w_three, *refs):
    pieces = refs[:count]
    outs = refs[count : 2 * count]
    key_t, target_o = refs[2 * count :]
    for p in range(count):
        k = pieces[p][0]
        v = pieces[p][1]
        rows = k.shape[0]
        at = slice(p * rows, (p + 1) * rows)
        t = (-piece_rate(idx, rate, p, k.shape[0]) * v.astype(f32)).astype(bf16)
        a_one = dot_nn(k, w_one[...])
        a_three = dot_nn(k, w_three[...])
        b = dot_nt(t, w_two[...])
        sq = sigmoid(a_one)
        swished = a_one * sq
        slope = sq * (1.0 + a_one * (1.0 - sq))
        slope_two = sq * (1.0 - sq) * (2.0 + a_one * (1.0 - 2.0 * sq))
        key_t[:, at] = k.T
        target_o[at] = t
        kept = (
            k,
            v,
            swished * a_three,
            b * a_three * slope,
            b * swished,
            a_three * slope,
            swished,
            b * slope,
            b * a_three * slope_two,
        )
        for j, value in enumerate(kept):
            outs[p][j] = value.astype(bf16)


def normalize_kernel(idx, mine, theirs, weight, update, stats, new):
    for j in range(3):
        w = weight[j]
        u = w - (mine[j].astype(f32) + theirs[j].astype(f32))
        ref_norm = jnp.sqrt(jnp.sum(w * w, axis=0, keepdims=True) + epsilon)
        upd_norm = jnp.sqrt(jnp.sum(u * u, axis=0, keepdims=True) + epsilon)
        update[j] = u
        stats[j, 0:1, :] = ref_norm
        stats[j, 1:2, :] = upd_norm
        new[j] = (u * (ref_norm / upd_norm)).astype(bf16)


def outer_piece(q, e, y, at, qt, eb, mt, d_one_b, d_three_b):
    c_one = dot_nn(q, y[0])
    c_three = dot_nn(q, y[2])
    dm = dot_nt(e, y[1])
    sq = sigmoid(c_one)
    swished = c_one * sq
    slope = sq * (1.0 + c_one * (1.0 - sq))
    qt[:, at] = q.T
    eb[at] = e
    mt[:, at] = (swished * c_three).astype(bf16).T
    d_one_b[at] = (dm * c_three * slope).astype(bf16)
    d_three_b[at] = (dm * swished).astype(bf16)


def apply_early_kernel(count, idx, y_own, y_other, *refs):
    pieces = refs[:count]
    qt, eb, mt, d_one_b, d_three_b, y = refs[count:]
    join_halves(idx, y_own, y_other, y)
    rows = pieces[0].shape[1]
    for p in range(count):
        at = slice(p * rows, (p + 1) * rows)
        outer_piece(pieces[p][0], pieces[p][1], y, at, qt, eb, mt, d_one_b, d_three_b)


def apply_late_kernel(count, idx, y_own, y_other, *refs):
    pieces, early = refs[:count], refs[count : count + 5]
    keep, send, d_one_b, d_three_b, qt, eb, mt, y = refs[count + 5 :]
    join_halves(idx, y_own, y_other, y)
    rows = pieces[0].shape[1]
    start = early[1].shape[0]
    qt[:, :start] = early[0][...]
    mt[:, :start] = early[2][...]
    for j, target in ((1, eb), (3, d_one_b), (4, d_three_b)):
        target[:start] = early[j][...]
    for p in range(count):
        at = slice(start + p * rows, start + (p + 1) * rows)
        outer_piece(pieces[p][0], pieces[p][1], y, at, qt, eb, mt, d_one_b, d_three_b)
    emit_halves(idx, ((qt, d_one_b), (mt, eb), (qt, d_three_b)), keep, send)


def query_kernel(count, idx, y_own, y_other, d_one, d_three, *refs):
    grads, y = refs[:count], refs[count]
    join_halves(idx, y_own, y_other, y)
    rows = grads[0].shape[1]
    for p in range(count):
        at = slice(p * rows, (p + 1) * rows)
        grads[p][0] = (dot_nt(d_one[at], y[0]) + dot_nt(d_three[at], y[2])).astype(bf16)


def adjoint_kernel(idx, mine, theirs, update, stats, cot, moments):
    for j in range(3):
        u = update[j]
        ref_norm = stats[j, 0:1, :]
        upd_norm = stats[j, 1:2, :]
        dy = mine[j].astype(f32) + theirs[j].astype(f32)
        moment = jnp.sum(dy * u, axis=0, keepdims=True)
        factor = ref_norm / upd_norm
        cot[j] = (u * (factor * moment / (upd_norm * upd_norm)) - factor * dy).astype(bf16)
        moments[j] = moment


def adjoint_piece(r, kept, g):
    k = kept[0]
    t = (-r * kept[1].astype(f32)).astype(bf16)
    f_one, f_two, f_three, f_four = [kept[j].astype(f32) for j in range(5, 9)]
    dd_one = dot_nn(k, g[0])
    dd_three = dot_nn(k, g[2])
    dh = dot_nt(t, g[1])
    db = (dd_one * f_one + dd_three * f_two).astype(bf16)
    da_three = (dd_one * f_three + dh * f_two).astype(bf16)
    da_one = (dd_one * f_four + dd_three * f_three + dh * f_one).astype(bf16)
    return da_one, db, da_three


def input_piece(r, kept, g, weights, da_one, db, da_three, grad, rate_grad, p):
    w_one, w_two, w_three = weights
    dt = dot_nn(kept[2], g[1]) + dot_nn(db, w_two[...])
    grad[0] = (
        (dot_nt(kept[3], g[0]) + dot_nt(kept[4], g[2]))
        + (dot_nt(da_one, w_one[...]) + dot_nt(da_three, w_three[...]))
    ).astype(bf16)
    grad[1] = (-r * dt).astype(bf16)
    rate_grad[p] = -jnp.sum(kept[1].astype(f32) * dt, axis=1, keepdims=True)


def double_last_kernel(piece, idx, rate, w_one, w_two, w_three, g_own, g_other, *refs):
    kept, grad, rate_grad, da_one_o, db_o, da_three_o, g = refs
    join_halves(idx, g_own, g_other, g)
    rows = da_one_o.shape[0]
    r = piece_rate(idx, rate, piece, rows)
    da_one, db, da_three = adjoint_piece(r, kept, g)
    da_one_o[...] = da_one
    db_o[...] = db
    da_three_o[...] = da_three
    weights = (w_one, w_two, w_three)
    input_piece(r, kept, g, weights, da_one, db, da_three, grad, rate_grad, 0)


def double_inner_kernel(count, idx, rate, g_own, g_other, *refs):
    kept = refs[:count]
    da_one_o, db_o, da_three_o, g = refs[count:]
    join_halves(idx, g_own, g_other, g)
    rows = kept[0].shape[1]
    for p in range(count):
        at = slice(p * rows, (p + 1) * rows)
        r = piece_rate(idx, rate, p, rows)
        da_one_o[at], db_o[at], da_three_o[at] = adjoint_piece(r, kept[p], g)


def double_input_kernel(base, count, idx, rate, w_one, w_two, w_three, g_own, g_other, *refs):
    da_one, db, da_three = refs[:3]
    kept, grads = refs[3 : 3 + count], refs[3 + count : 3 + 2 * count]
    rate_grad, g = refs[3 + 2 * count :]
    join_halves(idx, g_own, g_other, g)
    rows = kept[0].shape[1]
    weights = (w_one, w_two, w_three)
    for p in range(count):
        at = slice((base + p) * rows, (base + p + 1) * rows)
        r = piece_rate(idx, rate, base + p, rows)
        input_piece(
            r, kept[p], g, weights, da_one[at], db[at], da_three[at], grads[p], rate_grad, p
        )


def weights_kernel(share, idx, key_t, target, *refs):
    mine, theirs, update, stats, moments, weight = refs[:6]
    first, last = refs[6:9], refs[9:12]
    keeps, sends = refs[12:14], refs[14:16]
    a_one_b, bt, a_three_b, direct = refs[16:]
    split = first[0].shape[0]
    for source, at in ((first, slice(0, split)), (last, slice(split, target.shape[0]))):
        a_one_b[at] = source[0][...]
        bt[:, at] = source[1][...].T
        a_three_b[at] = source[2][...]
    for j in range(3):
        ref_norm = stats[j, 0:1, :]
        upd_norm = stats[j, 1:2, :]
        moment = moments[j]
        factor = ref_norm / upd_norm
        dy = mine[j].astype(f32) + theirs[j].astype(f32)
        du = factor * dy - update[j] * (factor * moment / (upd_norm * upd_norm))
        direct[j] = (weight[j] * (moment / (upd_norm * ref_norm)) + du) * share
    half = weight.shape[2]
    rows = keeps[0].shape[1]
    own, other = columns(idx, half)
    pairs = ((key_t, a_one_b), (bt, target), (key_t, a_three_b))
    for j, (left, right) in enumerate(pairs):
        total = dot_nn(left[...], right[:, pl.ds(other, half)]).astype(bf16)
        sends[0][j] = total[:rows]
        sends[1][j] = total[rows:]
    for j, (left, right) in enumerate(pairs):
        total = dot_nn(left[...], right[:, pl.ds(own, half)]) + direct[j]
        keeps[0][j] = total[:rows]
        keeps[1][j] = total[rows:]


def join_kernel(count, idx, *refs):
    sides, outs = (refs[:count], refs[count : 2 * count]), refs[2 * count :]
    half = refs[0].shape[2]
    for lanes, parts in zip(columns(idx, half), sides):
        row = 0
        for part in parts:
            rows = part.shape[1]
            for j in range(3):
                outs[j][row : row + rows, pl.ds(lanes, half)] = part[j].astype(f32)
            row += rows


def paste_kernel(count, idx, *refs):
    pieces, outs = refs[:count], refs[count:]
    width = pieces[0].shape[-1]
    for p in range(count):
        lanes = pl.ds(pl.multiple_of((idx[0] ^ p) * width, width), width)
        for side, out in enumerate(outs):
            out[:, lanes] = pieces[p][side]


def call(kernel, operands, outs, scratch=()):
    smem = pl.BlockSpec(memory_space=pltpu.SMEM)
    vmem = pl.BlockSpec(memory_space=pltpu.VMEM)
    return pl.pallas_call(
        kernel,
        out_shape=outs,
        in_specs=[smem] + [vmem] * (len(operands) - 1),
        out_specs=[vmem] * len(outs),
        scratch_shapes=scratch,
    )(*operands)


def shape(dims, dtype):
    return jax.ShapeDtypeStruct(tuple(dims), dtype)


def xor_permute(x, axis, bit):
    size = lax.axis_size(axis)
    return lax.ppermute(x, axis, [(i, i ^ bit) for i in range(size)])


def body(queries, keys, values, rates, fast_one, fast_two, fast_three, grad_out):
    count = lax.axis_size("head")
    tok = lax.axis_size("tok")
    rows = keys.shape[1]
    fan_in, hidden_units = fast_one.shape[1], fast_one.shape[2]
    width = fan_in
    half = hidden_units // 2
    early = count // 2
    late = count - early
    head = lax.axis_index("head").astype(jnp.int32)
    core = lax.axis_index("tok").astype(jnp.int32) & 1
    idx = jnp.stack([head, core])
    weights = (fast_one[0], fast_two[0], fast_three[0])
    low = tuple(w.astype(bf16) for w in weights)
    weight_half = jnp.stack(
        [lax.dynamic_slice(w, (0, core * half), (fan_in, half)) for w in weights]
    )
    rate = rates.reshape(-1, 1)

    def exchange(pieces, first=1):
        return [
            piece if p == 0 else xor_permute(piece, "head", p)
            for p, piece in enumerate(pieces, first)
        ]

    def paste(pieces):
        out = shape((rows, count * width), bf16)
        sides = pieces[0].shape[0]
        kernel = functools.partial(paste_kernel, count)
        return [x[None] for x in call(kernel, (idx, *pieces), [out] * sides)]

    def tok_exchange(keep, sent):
        mine = (keep + sent.astype(f32)).astype(bf16)
        bit = 2
        theirs = xor_permute(mine, "tok", bit)
        while bit * 2 < tok:
            bit *= 2
            mine = (mine.astype(f32) + theirs.astype(f32)).astype(bf16)
            theirs = xor_permute(mine, "tok", bit)
        return mine, theirs

    block = (3, fan_in, half)
    halves = [shape(block, f32), shape(block, bf16)]
    square = (3, fan_in, hidden_units)
    tokens = count * rows
    tall = (tokens, width)
    flat = (width, tokens)
    both = shape((2, rows, width), bf16)

    kv_cut = call(cut_kernel, (idx, keys[0], values[0]), [both] * count)
    qe_cut = call(cut_kernel, (idx, queries[0], grad_out[0]), [both] * count)
    kv = exchange(kv_cut, 0)
    qe = [qe_cut[0]]
    for p in range(1, count):
        kv[p], piece = lax.optimization_barrier((kv[p], qe_cut[p]))
        qe.append(xor_permute(piece, "head", p))

    keep, send = call(
        functools.partial(inner_kernel, count),
        (idx, rate, *low, *kv),
        halves,
        [pltpu.VMEM(flat, bf16), pltpu.VMEM(tall, bf16)] * 2 + [pltpu.VMEM(tall, bf16)],
    )
    idx_late, send = lax.optimization_barrier((idx, send))
    mine, theirs = tok_exchange(keep, xor_permute(send, "tok", 1))
    stack = shape((9, rows, width), bf16)
    *kept, key_t, target = call(
        functools.partial(factor_kernel, count),
        (idx_late, rate, *low, *kv),
        [stack] * count + [shape(flat, bf16), shape(tall, bf16)],
    )
    update, stats, y_own = call(
        normalize_kernel,
        (idx, mine, theirs, weight_half),
        [shape(block, f32), shape((3, 2, half), f32), shape(block, bf16)],
    )
    y_other = xor_permute(y_own, "tok", 1)
    begun = call(
        functools.partial(apply_early_kernel, early),
        (idx, y_own, y_other, *qe[:early]),
        [shape((width, early * rows), bf16), shape((early * rows, width), bf16)] * 2
        + [shape((early * rows, width), bf16)],
        [pltpu.VMEM(square, bf16)],
    )
    keep, send, d_one, d_three = call(
        functools.partial(apply_late_kernel, late),
        (idx, y_own, y_other, *qe[early:], *begun),
        halves + [shape(tall, bf16)] * 2,
        [
            pltpu.VMEM(flat, bf16),
            pltpu.VMEM(tall, bf16),
            pltpu.VMEM(flat, bf16),
            pltpu.VMEM(square, bf16),
        ],
    )
    mine, theirs = tok_exchange(keep, xor_permute(send, "tok", 1))
    grad_q = call(
        functools.partial(query_kernel, count),
        (idx, y_own, y_other, d_one, d_three),
        [shape((1, rows, width), bf16)] * count,
        [pltpu.VMEM(square, bf16)],
    )
    (query_back,) = paste(exchange(grad_q, 0))
    cot_own, moment = call(
        adjoint_kernel,
        (idx, mine, theirs, update, stats),
        [shape(block, bf16), shape((3, 1, half), f32)],
    )
    cot_other = xor_permute(cot_own, "tok", 1)

    cots = (cot_own, cot_other)
    joined = [pltpu.VMEM(square, bf16)]
    final = count - 1
    grad, last_rate, *last = call(
        functools.partial(double_last_kernel, final),
        (idx, rate, *low, *cots, kept[final]),
        [both, shape((1, rows, 1), f32)] + [shape((rows, width), bf16)] * 3,
        joined,
    )
    kv_back = [None] * final + exchange([grad], final)
    inner_cots = call(
        functools.partial(double_inner_kernel, final),
        (idx, rate, *cots, *kept[:final]),
        [shape((final * rows, width), bf16)] * 3,
        joined,
    )
    cut_row = fan_in // 2
    part_block = (3, cut_row, half)
    results = call(
        functools.partial(weights_kernel, 2.0 / tok),
        (
            idx, key_t, target, mine, theirs, update, stats, moment, weight_half,
            *inner_cots, *last,
        ),
        [shape(part_block, f32)] * 2 + [shape(part_block, bf16)] * 2,
        [
            pltpu.VMEM(tall, bf16),
            pltpu.VMEM(flat, bf16),
            pltpu.VMEM(tall, bf16),
            pltpu.VMEM(block, f32),
        ],
    )
    rate_parts = [last_rate]
    for base, span in [(p, 1) for p in reversed(range(early, final))] + [(0, early)]:
        res = call(
            functools.partial(double_input_kernel, base, span),
            (idx, rate, *low, *cots, *inner_cots, *kept[base : base + span]),
            [both] * span + [shape((span, rows, 1), f32)],
            joined,
        )
        kv_back[base : base + span] = exchange(res[:span], base)
        rate_parts = [res[span], *rate_parts]
    key_back, value_back = paste(kv_back)
    rate_grad = jnp.concatenate(rate_parts, axis=0).reshape(count, rows)
    rate_grad = rate_grad[jnp.arange(count) ^ head]

    chips = [
        keep + xor_permute(send, "tok", 1).astype(f32)
        for keep, send in zip(results[:2], results[2:])
    ]
    stages = [("tok", 1 << b) for b in range(1, tok.bit_length() - 1)]
    stages_seq = [("seq", 1 << b) for b in range(lax.axis_size("seq").bit_length() - 1)]
    parts = []
    for part, order in ((chips[0], stages + stages_seq), (chips[1], stages_seq + stages)):
        for axis, bit in order:
            part = part.astype(bf16)
            moved = xor_permute(part, axis, bit)
            part = part.astype(f32) + moved.astype(f32)
        parts.append(part.astype(bf16))
    others = [xor_permute(x, "tok", 1) for x in parts]
    totals = call(
        functools.partial(join_kernel, len(parts)),
        (idx, *parts, *others),
        [shape((fan_in, hidden_units), f32)] * 3,
    )
    rate_grads = rate_grad.reshape(rates.shape)
    return (query_back, key_back, value_back, rate_grads, *(t[None] for t in totals))


def solution(mesh):
    tokens = P("seq", ("tok", "head"), None)
    placed = (
        tokens,
        tokens,
        tokens,
        P("seq", "head", "tok"),
        P("head", None, None),
        P("head", None, None),
        P("head", None, None),
        tokens,
    )
    return jax.shard_map(
        body,
        mesh=mesh,
        in_specs=placed,
        out_specs=(
            tokens,
            tokens,
            tokens,
            P("seq", "head", "tok"),
            P("head", None, None),
            P("head", None, None),
            P("head", None, None),
        ),
        check_vma=False,
    )
```

time: 297 us -> 304 us (1.024)
  the two profiles are of different devices: /device:TPU:0 before, /device:TPU:8 now
where the time goes in v1:
time: 304 us; the launch traced here: 303 us
  waiting for transfers between devices  174 us (57%)
  Pallas kernels  84.3 us (28%)
  starting transfers between devices  24.2 us (8%)
  local copies, waits for them, and re-layouts  11.5 us (4%)
  other arithmetic  8.79 us (3%)
    ppermute x26, waiting for transfers between devices, xor_permute(): return lax.ppermute(x, axis, [(i, i ^ bit) for i in range(size)])  174 us
    pallas_call x17, Pallas kernels, call(): pl.pallas_call(kernel, out_shape=outs, in_specs=[smem] + [vmem] * (len(op...  84.3 us
    ppermute x26, starting transfers between devices, xor_permute(): return lax.ppermute(x, axis, [(i, i ^ bit) for i in range(size)])  24.2 us
  transfers between devices with their start and end apart: 26, of which 17 were waited for; matrix products, arithmetic and copies ran while one was open for 3% of the time, Pallas kernels for 12%

profile of v1, /device:TPU:8, one launch (start us, length us, event | category | flops | bytes accessed | tf_op | source)
XLA Modules:
  0.0 303.2 jit_solution(14031447121482699944)
XLA Ops:
  0.6 0.6 pad_add_fusion.idx
  1.2 3.0 shard_map.135
  4.3 3.0 %collective-permute-start.1 = (bf16[2,256,512]{2,1,0:T(8,128)(2,1)}, bf16[2,256,512]{2,1,0:T(8,128)(2,1)}, u32[]{:S(2)}, u32[]{:S(2)}) collective-permute-start(bf16[2,256,512]{2,1,0:T(8,128)(2,1)} %get-tuple-element.75), channel_id=1, source_target_pairs={{0,4},{2,6},{4,0},{6,2},{1,5},{3,7},{5,1},{7,3},{8,12},{10,14},{12... | collective-permute-start | bytes 1572872 | tf_op jit(solution)/shard_map/ppermute | solution.py:327
  7.8 1.0 copy.21.rate
  8.8 3.2 %shard_map.136 = (bf16[2,256,512]{2,1,0:T(8,128)(2,1)}, bf16[2,256,512]{2,1,0:T(8,128)(2,1)}, bf16[2,256,512]{2,1,0:T(8,128)(2,1)}, bf16[2,256,512]{2,1,0:T(8,128)(2,1)}) custom-call(s32[2]{0:T(128)} %pad_add_fusion.idx, bf16[256,2048]{1,0:T(8,128)(2,1)} %bitcast.25, bf16[256,2048]{1,0:T(8,128)(2,1)} %bitcast.26), custom_call_target="tpu_custom_call" | custom-call | tf_op jit(solution)/shard_map/pallas_call | solution.py:312
  12.0 0.9 convert_bitcast_fusion.2.w_one
  12.8 1.1 convert_bitcast_fusion
  14.0 12.6 %collective-permute-done.refs_1_ = bf16[2,256,512]{2,1,0:T(8,128)(2,1)} collective-permute-done((bf16[2,256,512]{2,1,0:T(8,128)(2,1)}, bf16[2,256,512]{2,1,0:T(8,128)(2,1)}, u32[]{:S(2)}, u32[]{:S(2)}) %collective-permute-start) | collective-permute-done | bytes 524320 | tf_op jit(solution)/shard_map/ppermute | solution.py:327
  26.5 15.9 %collective-permute-done.1.refs_2_ = bf16[2,256,512]{2,1,0:T(8,128)(2,1)} collective-permute-done((bf16[2,256,512]{2,1,0:T(8,128)(2,1)}, bf16[2,256,512]{2,1,0:T(8,128)(2,1)}, u32[]{:S(2)}, u32[]{:S(2)}) %collective-permute-start.1) | collective-permute-done | bytes 524320 | tf_op jit(solution)/shard_map/ppermute | solution.py:327
  42.4 10.8 %collective-permute-done.2.refs_3_ = bf16[2,256,512]{2,1,0:T(8,128)(2,1)} collective-permute-done((bf16[2,256,512]{2,1,0:T(8,128)(2,1)}, bf16[2,256,512]{2,1,0:T(8,128)(2,1)}, u32[]{:S(2)}, u32[]{:S(2)}) %collective-permute-start.2) | collective-permute-done | bytes 524320 | tf_op jit(solution)/shard_map/ppermute | solution.py:327
  53.2 7.5 %shard_map.137 = (f32[3,512,256]{2,1,0:T(8,128)}, bf16[3,512,256]{2,1,0:T(8,128)(2,1)}) custom-call(s32[2]{0:T(128)} %pad_add_fusion.idx, f32[1024,1]{1,0:T(8,128)} %copy.21.rate, bf16[512,512]{1,0:T(8,128)(2,1)} %convert_bitcast_fusion.2.w_one, bf16[512,512]{1,0:T(8,128)(2,1)} %get-tuple-element.136.w_two, bf16[512,512]{1,0:T(8,128)(2,1)} %get-tuple-element.135.w_three, ...), custom_call_target="tpu_custom_call" | custom-call | tf_op jit(solution)/shard_map/pallas_call | solution.py:312
  60.7 2.5 collective-permute-done.3
  63.2 1.6 add_convert_fusion.1.mine
  64.8 1.6 collective-permute-start.4
  66.4 1.1 constant_dynamic-slice_fusion.2
  67.6 1.3 pad_maximum_fusion.weight.refs_5_
  68.9 15.7 %collective-permute-done.4.theirs = bf16[3,512,256]{2,1,0:T(8,128)(2,1)} collective-permute-done((bf16[3,512,256]{2,1,0:T(8,128)(2,1)S(1)}, bf16[3,512,256]{2,1,0:T(8,128)(2,1)}, u32[]{:S(2)}, u32[]{:S(2)}) %collective-permute-start.4) | collective-permute-done | bytes 786464 | tf_op jit(solution)/shard_map/ppermute | solution.py:327
  84.6 4.0 %shard_map.138 = (f32[3,512,256]{2,1,0:T(8,128)}, f32[3,2,256]{2,1,0:T(2,128)}, bf16[3,512,256]{2,1,0:T(8,128)(2,1)}) custom-call(s32[2]{0:T(128)} %pad_add_fusion.idx, bf16[3,512,256]{2,1,0:T(8,128)(2,1)} %copy-done.4, bf16[3,512,256]{2,1,0:T(8,128)(2,1)} %collective-permute-done.4.theirs, f32[3,512,256]{2,1,0:T(8,128)} %pad_maximum_fusion.weight.refs_5_), custom_call_target="tpu_custom_call" | custom-call | tf_op jit(solution)/shard_map/pallas_call | solution.py:312
  88.6 3.0 %collective-permute-start.6 = (bf16[2,256,512]{2,1,0:T(8,128)(2,1)}, bf16[2,256,512]{2,1,0:T(8,128)(2,1)S(1)}, u32[]{:S(2)}, u32[]{:S(2)}) collective-permute-start(bf16[2,256,512]{2,1,0:T(8,128)(2,1)} %get-tuple-element.85), channel_id=1, source_target_pairs={{0,4},{2,6},{4,0},{6,2},{1,5},{3,7},{5,1},{7,3},{8,12},{10,14},{12... | collective-permute-start | bytes 1572872 | tf_op jit(solution)/shard_map/ppermute | solution.py:327
  92.1 19.8 %collective-permute-done.8.refs_1_ = bf16[2,256,512]{2,1,0:T(8,128)(2,1)S(1)} collective-permute-done((bf16[2,256,512]{2,1,0:T(8,128)(2,1)}, bf16[2,256,512]{2,1,0:T(8,128)(2,1)S(1)}, u32[]{:S(2)}, u32[]{:S(2)}) %collective-permute-start.8) | collective-permute-done | bytes 524320 | tf_op jit(solution)/shard_map/ppermute | solution.py:327
  111.9 0.8 copy-done.14
  112.9 4.3 %shard_map.139 = (bf16[512,512]{1,0:T(8,128)(2,1)}, bf16[512,512]{1,0:T(8,128)(2,1)}, bf16[512,512]{1,0:T(8,128)(2,1)}, bf16[512,512]{1,0:T(8,128)(2,1)}, bf16[512,512]{1,0:T(8,128)(2,1)}) custom-call(s32[2]{0:T(128)} %pad_add_fusion.idx, bf16[3,512,256]{2,1,0:T(8,128)(2,1)} %get-tuple-element.84.y_own, bf16[3,512,256]{2,1,0:T(8,128)(2,1)} %copy-done.2, ...), custom_call_target="tpu_custom_call" | custom-call | tf_op jit(solution)/shard_map/pallas_call | solution.py:312
  117.2 9.6 %collective-permute-done.6.refs_0_ = bf16[2,256,512]{2,1,0:T(8,128)(2,1)S(1)} collective-permute-done((bf16[2,256,512]{2,1,0:T(8,128)(2,1)}, bf16[2,256,512]{2,1,0:T(8,128)(2,1)S(1)}, u32[]{:S(2)}, u32[]{:S(2)}) %collective-permute-start.6) | collective-permute-done | bytes 524320 | tf_op jit(solution)/shard_map/ppermute | solution.py:327
  126.8 11.3 %collective-permute-done.7.refs_1_ = bf16[2,256,512]{2,1,0:T(8,128)(2,1)S(1)} collective-permute-done((bf16[2,256,512]{2,1,0:T(8,128)(2,1)S(1)}, bf16[2,256,512]{2,1,0:T(8,128)(2,1)S(1)}, u32[]{:S(2)}, u32[]{:S(2)}) %collective-permute-start.7) | collective-permute-done | bytes 524320 | tf_op jit(solution)/shard_map/ppermute | solution.py:327
  138.1 0.8 copy-done.16
  138.9 6.8 %shard_map.140 = (f32[3,512,256]{2,1,0:T(8,128)}, bf16[3,512,256]{2,1,0:T(8,128)(2,1)}, bf16[1024,512]{1,0:T(8,128)(2,1)}, bf16[1024,512]{1,0:T(8,128)(2,1)}) custom-call(s32[2]{0:T(128)} %pad_add_fusion.idx, bf16[3,512,256]{2,1,0:T(8,128)(2,1)} %get-tuple-element.84.y_own, bf16[3,512,256]{2,1,0:T(8,128)(2,1)} %copy-done.2, bf16[2,256,512]{2,1,0:T(8,128)(2,1)} %copy-done.15, ...), custom_call_target="tpu_custom_call" | custom-call | tf_op jit(solution)/shard_map/pallas_call | solution.py:312
  145.7 2.5 collective-permute-done.12
  148.2 1.6 add_convert_fusion.mine.refs_0_
  149.9 1.6 collective-permute-start.13
  151.4 18.1 %collective-permute-done.13.theirs.refs_1_ = bf16[3,512,256]{2,1,0:T(8,128)(2,1)S(1)} collective-permute-done((bf16[3,512,256]{2,1,0:T(8,128)(2,1)S(1)}, bf16[3,512,256]{2,1,0:T(8,128)(2,1)S(1)}, u32[]{:S(2)}, u32[]{:S(2)}) %collective-permute-start.13) | collective-permute-done | bytes 786464 | tf_op jit(solution)/shard_map/ppermute | solution.py:327
  169.5 0.9 copy-done.3
  170.4 3.3 %shard_map.143 = (bf16[3,512,256]{2,1,0:T(8,128)(2,1)}, f32[3,1,256]{2,1,0:T(1,128)}) custom-call(s32[2]{0:T(128)} %pad_add_fusion.idx, bf16[3,512,256]{2,1,0:T(8,128)(2,1)} %copy-done.1, bf16[3,512,256]{2,1,0:T(8,128)(2,1)} %copy-done.3, f32[3,512,256]{2,1,0:T(8,128)} %get-tuple-element.102.update.refs_2_, f32[3,2,256]{2,1,0:T(2,128)} %get-tuple-element.103.stats.refs_3_), custom_call_target="tpu_custom_call" | custom-call | tf_op jit(solution)/shard_map/pallas_call | solution.py:312
  173.7 7.7 %shard_map.144 = (bf16[9,256,512]{2,1,0:T(8,128)(2,1)}, bf16[9,256,512]{2,1,0:T(8,128)(2,1)}, bf16[9,256,512]{2,1,0:T(8,128)(2,1)}, bf16[9,256,512]{2,1,0:T(8,12...) custom-call(s32[2]{0:T(128)} %pad_add_fusion.idx, f32[1024,1]{1,0:T(8,128)} %copy.21.rate, ...), custom_call_target="tpu_custom_call" | custom-call | tf_op jit(solution)/shard_map/pallas_call | solution.py:312
  181.5 0.9 copy-done
  182.4 5.3 %shard_map.148 = (bf16[2,256,512]{2,1,0:T(8,128)(2,1)}, f32[1,256,1]{2,1,0:T(8,128)}, bf16[256,512]{1,0:T(8,128)(2,1)}, bf16[256,512]{1,0:T(8,128)(2,1)}, bf16[256,512]{1,0:T(8,128)(2,1)}) custom-call(s32[2]{0:T(128)} %pad_add_fusion.idx, f32[1024,1]{1,0:T(8,128)} %copy.21.rate, bf16[512,512]{1,0:T(8,128)(2,1)} %convert_bitcast_fusion.2.w_one, ...), custom_call_target="tpu_custom_call" | custom-call | tf_op jit(solution)/shard_map/pallas_call | solution.py:312
  187.7 7.2 %shard_map.145 = (bf16[768,512]{1,0:T(8,128)(2,1)}, bf16[768,512]{1,0:T(8,128)(2,1)}, bf16[768,512]{1,0:T(8,128)(2,1)}) custom-call(s32[2]{0:T(128)} %pad_add_fusion.idx, f32[1024,1]{1,0:T(8,128)} %copy.21.rate, bf16[3,512,256]{2,1,0:T(8,128)(2,1)} %get-tuple-element.104.g_own, bf16[3,512,256]{2,1,0:T(8,128)(2,1)} %copy-done, ...), custom_call_target="tpu_custom_call" | custom-call | tf_op jit(solution)/shard_map/pallas_call | solution.py:312
  194.9 7.0 %shard_map.150 = (f32[3,256,256]{2,1,0:T(8,128)}, f32[3,256,256]{2,1,0:T(8,128)}, bf16[3,256,256]{2,1,0:T(8,128)(2,1)}, bf16[3,256,256]{2,1,0:T(8,128)(2,1)}) custom-call(s32[2]{0:T(128)} %pad_add_fusion.idx, bf16[512,1024]{1,0:T(8,128)(2,1)} %get-tuple-element.122.key_t, bf16[1024,512]{1,0:T(8,128)(2,1)} %get-tuple-element.123.target, ...), custom_call_target="tpu_custom_call" | custom-call | tf_op jit(solution)/shard_map/pallas_call | solution.py:312
  202.6 1.5 collective-permute-done.18
  204.1 1.2 add_convert_fusion.7
  205.3 1.6 collective-permute-start.19
  207.0 1.6 collective-permute-start.22
  208.6 8.2 %collective-permute-done.19 = bf16[3,256,256]{2,1,0:T(8,128)(2,1)S(1)} collective-permute-done((bf16[3,256,256]{2,1,0:T(8,128)(2,1)S(1)}, bf16[3,256,256]{2,1,0:T(8,128)(2,1)S(1)}, u32[]{:S(2)}, u32[]{:S(2)}) %collective-permute-start.19) | collective-permute-done | bytes 393248 | tf_op jit(solution)/shard_map/ppermute | solution.py:327
  216.9 1.6 collective-permute-start.20
  218.6 1.6 collective-permute-start.23
  220.2 4.1 %shard_map.141 = (bf16[1,256,512]{2,1,0:T(8,128)(2,1)}, bf16[1,256,512]{2,1,0:T(8,128)(2,1)}, bf16[1,256,512]{2,1,0:T(8,128)(2,1)}, bf16[1,256,512]{2,1,0:T(8,128)(2,1)}) custom-call(s32[2]{0:T(128)} %pad_add_fusion.idx, bf16[3,512,256]{2,1,0:T(8,128)(2,1)} %get-tuple-element.84.y_own, bf16[3,512,256]{2,1,0:T(8,128)(2,1)} %copy-done.2, ...), custom_call_target="tpu_custom_call" | custom-call | tf_op jit(solution)/shard_map/pallas_call | solution.py:312
  224.3 3.0 collective-permute-start.10
  227.8 6.9 %shard_map.146 = (bf16[2,256,512]{2,1,0:T(8,128)(2,1)}, bf16[2,256,512]{2,1,0:T(8,128)(2,1)}, f32[2,256,1]{2,1,0:T(8,128)}) custom-call(s32[2]{0:T(128)} %pad_add_fusion.idx, f32[1024,1]{1,0:T(8,128)} %copy.21.rate, bf16[512,512]{1,0:T(8,128)(2,1)} %convert_bitcast_fusion.2.w_one, bf16[512,512]{1,0:T(8,128)(2,1)} %get-tuple-element.136.w_two, ...), custom_call_target="tpu_custom_call" | custom-call | tf_op jit(solution)/shard_map/pallas_call | solution.py:312
  234.7 5.4 %shard_map.147 = (bf16[2,256,512]{2,1,0:T(8,128)(2,1)}, f32[1,256,1]{2,1,0:T(8,128)}) custom-call(s32[2]{0:T(128)} %pad_add_fusion.idx, f32[1024,1]{1,0:T(8,128)} %copy.21.rate, bf16[512,512]{1,0:T(8,128)(2,1)} %convert_bitcast_fusion.2.w_one, bf16[512,512]{1,0:T(8,128)(2,1)} %get-tuple-element.136.w_two, bf16[512,512]{1,0:T(8,128)(2,1)} %get-tuple-element.135.w_three, ...), custom_call_target="tpu_custom_call" | custom-call | tf_op jit(solution)/shard_map/pallas_call | solution.py:312
  240.1 1.1 collective-permute-start.15
  241.3 2.1 collective-permute-start.16
  243.9 1.6 collective-permute-done.10.refs_2_
  245.5 6.5 %collective-permute-done.11.refs_3_ = bf16[1,256,512]{2,1,0:T(8,128)(2,1)} collective-permute-done((bf16[1,256,512]{2,1,0:T(8,128)(2,1)}, bf16[1,256,512]{2,1,0:T(8,128)(2,1)}, u32[]{:S(2)}, u32[]{:S(2)}) %collective-permute-start.11) | collective-permute-done | bytes 262176 | tf_op jit(solution)/shard_map/ppermute | solution.py:327
  252.1 2.2 shard_map.142
  254.5 1.0 copy.28
  255.4 1.1 copy.27
  257.1 0.6 reshape.50
  257.7 3.3 %collective-permute-done.15.refs_1_ = bf16[2,256,512]{2,1,0:T(8,128)(2,1)S(1)} collective-permute-done((bf16[2,256,512]{2,1,0:T(8,128)(2,1)}, bf16[2,256,512]{2,1,0:T(8,128)(2,1)S(1)}, u32[]{:S(2)}, u32[]{:S(2)}) %collective-permute-start.15) | collective-permute-done | bytes 524320 | tf_op jit(solution)/shard_map/ppermute | solution.py:327
  261.0 23.9 %collective-permute-done.16.refs_2_ = bf16[2,256,512]{2,1,0:T(8,128)(2,1)S(1)} collective-permute-done((bf16[2,256,512]{2,1,0:T(8,128)(2,1)}, bf16[2,256,512]{2,1,0:T(8,128)(2,1)S(1)}, u32[]{:S(2)}, u32[]{:S(2)}) %collective-permute-start.16) | collective-permute-done | bytes 524320 | tf_op jit(solution)/shard_map/ppermute | solution.py:327
  284.9 9.9 %collective-permute-done.17.refs_3_ = bf16[2,256,512]{2,1,0:T(8,128)(2,1)S(1)} collective-permute-done((bf16[2,256,512]{2,1,0:T(8,128)(2,1)}, bf16[2,256,512]{2,1,0:T(8,128)(2,1)S(1)}, u32[]{:S(2)}, u32[]{:S(2)}) %collective-permute-start.17) | collective-permute-done | bytes 524320 | tf_op jit(solution)/shard_map/ppermute | solution.py:327
  294.7 0.8 copy-done.13
  295.5 3.0 shard_map.149
  298.5 0.7 copy-done.17
  299.3 0.7 copy-done.18
  300.0 3.2 %shard_map.151 = (f32[512,512]{1,0:T(8,128)}, f32[512,512]{1,0:T(8,128)}, f32[512,512]{1,0:T(8,128)}) custom-call(s32[2]{0:T(128)} %pad_add_fusion.idx, bf16[3,256,256]{2,1,0:T(8,128)(2,1)} %copy-done.8, bf16[3,256,256]{2,1,0:T(8,128)(2,1)} %copy-done.9, bf16[3,256,256]{2,1,0:T(8,128)(2,1)} %copy-done.17, bf16[3,256,256]{2,1,0:T(8,128)(2,1)} %copy-done.18), custom_call_target="tpu_custom_call" | custom-call | tf_op jit(solution)/shard_map/pallas_call | solution.py:312
  (74 shorter events, 4.1 us)
Async XLA Ops:
  0.6 7.1 %copy-start.21 = (f32[1,1,1024]{2,1,0:T(1,128)S(1)}, f32[1,1,1024]{2,1,0:T(1,128)}, u32[]{:S(2)}) copy-start(f32[1,1,1024]{2,1,0:T(1,128)} %param.11) | copy-start | bytes 12292
  4.3 7.7 %copy-start.7 = (f32[1,512,512]{2,1,0:T(8,128)S(1)}, f32[1,512,512]{2,1,0:T(8,128)}, u32[]{:S(2)}) copy-start(f32[1,512,512]{2,1,0:T(8,128)} %param.12) | copy-start | bytes 3145732
  4.3 22.3 %collective-permute-start = (bf16[2,256,512]{2,1,0:T(8,128)(2,1)}, bf16[2,256,512]{2,1,0:T(8,128)(2,1)}, u32[]{:S(2)}, u32[]{:S(2)}) collective-permute-start(bf16[2,256,512]{2,1,0:T(8,128)(2,1)} %get-tuple-element.72), channel_id=1, source_target_pairs={{0,2},{2,0},{4,6},{6,4},{1,3},{3,1},{5,7},{7,5},{8,10},{10,8},{12,... | collective-permute-start | bytes 1572872 | tf_op jit(solution)/shard_map/ppermute | solution.py:327
  4.3 38.1 %collective-permute-start.1 = (bf16[2,256,512]{2,1,0:T(8,128)(2,1)}, bf16[2,256,512]{2,1,0:T(8,128)(2,1)}, u32[]{:S(2)}, u32[]{:S(2)}) collective-permute-start(bf16[2,256,512]{2,1,0:T(8,128)(2,1)} %get-tuple-element.75), channel_id=1, source_target_pairs={{0,4},{2,6},{4,0},{6,2},{1,5},{3,7},{5,1},{7,3},{8,12},{10,14},{12... | collective-permute-start | bytes 1572872 | tf_op jit(solution)/shard_map/ppermute | solution.py:327
  7.3 45.9 %collective-permute-start.2 = (bf16[2,256,512]{2,1,0:T(8,128)(2,1)}, bf16[2,256,512]{2,1,0:T(8,128)(2,1)}, u32[]{:S(2)}, u32[]{:S(2)}) collective-permute-start(bf16[2,256,512]{2,1,0:T(8,128)(2,1)} %get-tuple-element.78), channel_id=1, source_target_pairs={{0,6},{2,4},{4,2},{6,0},{1,7},{3,5},{5,3},{7,1},{8,14},{10,12},{12... | collective-permute-start | bytes 1572872 | tf_op jit(solution)/shard_map/ppermute | solution.py:327
  8.8 4.0 %copy-start.5 = (f32[1,512,512]{2,1,0:T(8,128)S(1)}, f32[1,512,512]{2,1,0:T(8,128)}, u32[]{:S(2)}) copy-start(f32[1,512,512]{2,1,0:T(8,128)} %param.14) | copy-start | bytes 3145732
  8.8 4.0 %copy-start.6 = (f32[1,512,512]{2,1,0:T(8,128)S(1)}, f32[1,512,512]{2,1,0:T(8,128)}, u32[]{:S(2)}) copy-start(f32[1,512,512]{2,1,0:T(8,128)} %param.13) | copy-start | bytes 3145732
  60.7 2.5 collective-permute-start.3
  64.8 2.8 copy-start.4
  64.8 19.8 %collective-permute-start.4 = (bf16[3,512,256]{2,1,0:T(8,128)(2,1)S(1)}, bf16[3,512,256]{2,1,0:T(8,128)(2,1)}, u32[]{:S(2)}, u32[]{:S(2)}) collective-permute-start(bf16[3,512,256]{2,1,0:T(8,128)(2,1)S(1)} %add_convert_fusion.1.mine), channel_id=1, source_target_pairs={{0,16},{8,24},{16,0},{24,8},{1,17},{9,25},{17,1},{25,9},{2,18},{10... | collective-permute-start | bytes 2359304 | tf_op jit(solution)/shard_map/ppermute | solution.py:327
  68.9 22.8 %copy-start.22 = (bf16[2,256,512]{2,1,0:T(8,128)(2,1)S(1)}, bf16[2,256,512]{2,1,0:T(8,128)(2,1)}, u32[]{:S(2)}) copy-start(bf16[2,256,512]{2,1,0:T(8,128)(2,1)} %get-tuple-element.86) | copy-start | bytes 1572868
  88.6 23.3 %collective-permute-start.5 = (bf16[3,512,256]{2,1,0:T(8,128)(2,1)}, bf16[3,512,256]{2,1,0:T(8,128)(2,1)S(1)}, u32[]{:S(2)}, u32[]{:S(2)}) collective-permute-start(bf16[3,512,256]{2,1,0:T(8,128)(2,1)} %get-tuple-element.84.y_own), channel_id=1, source_target_pairs={{0,8},{8,0},{16,24},{24,16},{1,9},{9,1},{17,25},{25,17},{2,10},{10... | collective-permute-start | bytes 2359304 | tf_op jit(solution)/shard_map/ppermute | solution.py:327
  88.6 23.3 %collective-permute-start.8 = (bf16[2,256,512]{2,1,0:T(8,128)(2,1)}, bf16[2,256,512]{2,1,0:T(8,128)(2,1)S(1)}, u32[]{:S(2)}, u32[]{:S(2)}) collective-permute-start(bf16[2,256,512]{2,1,0:T(8,128)(2,1)} %get-tuple-element.88), channel_id=1, source_target_pairs={{0,2},{2,0},{4,6},{6,4},{1,3},{3,1},{5,7},{7,5},{8,10},{10,8},{12,... | collective-permute-start | bytes 1572872 | tf_op jit(solution)/shard_map/ppermute | solution.py:327
  88.6 38.2 %collective-permute-start.6 = (bf16[2,256,512]{2,1,0:T(8,128)(2,1)}, bf16[2,256,512]{2,1,0:T(8,128)(2,1)S(1)}, u32[]{:S(2)}, u32[]{:S(2)}) collective-permute-start(bf16[2,256,512]{2,1,0:T(8,128)(2,1)} %get-tuple-element.85), channel_id=1, source_target_pairs={{0,4},{2,6},{4,0},{6,2},{1,5},{3,7},{5,1},{7,3},{8,12},{10,14},{12... | collective-permute-start | bytes 1572872 | tf_op jit(solution)/shard_map/ppermute | solution.py:327
  91.7 46.4 %collective-permute-start.7 = (bf16[2,256,512]{2,1,0:T(8,128)(2,1)S(1)}, bf16[2,256,512]{2,1,0:T(8,128)(2,1)S(1)}, u32[]{:S(2)}, u32[]{:S(2)}) collective-permute-start(bf16[2,256,512]{2,1,0:T(8,128)(2,1)S(1)} %copy-done.22), channel_id=1, source_target_pairs={{0,6},{2,4},{4,2},{6,0},{1,7},{3,5},{5,3},{7,1},{8,14},{10,12},{12... | collective-permute-start | bytes 1572872 | tf_op jit(solution)/shard_map/ppermute | solution.py:327
  111.9 0.8 copy-start.14
  111.9 1.0 copy-start.2
  126.8 11.3 %copy-start.15 = (bf16[2,256,512]{2,1,0:T(8,128)(2,1)}, bf16[2,256,512]{2,1,0:T(8,128)(2,1)S(1)}, u32[]{:S(2)}) copy-start(bf16[2,256,512]{2,1,0:T(8,128)(2,1)S(1)} %collective-permute-done.6.refs_0_) | copy-start | bytes 1572868
  138.1 0.8 copy-start.16
  145.7 2.5 collective-permute-start.12
  149.8 19.7 %copy-start.1 = (bf16[3,512,256]{2,1,0:T(8,128)(2,1)}, bf16[3,512,256]{2,1,0:T(8,128)(2,1)S(1)}, u32[]{:S(2)}) copy-start(bf16[3,512,256]{2,1,0:T(8,128)(2,1)S(1)} %add_convert_fusion.mine.refs_0_) | copy-start | bytes 2359300
  149.9 19.6 %collective-permute-start.13 = (bf16[3,512,256]{2,1,0:T(8,128)(2,1)S(1)}, bf16[3,512,256]{2,1,0:T(8,128)(2,1)S(1)}, u32[]{:S(2)}, u32[]{:S(2)}) collective-permute-start(bf16[3,512,256]{2,1,0:T(8,128)(2,1)S(1)} %add_convert_fusion.mine.refs_0_), channel_id=1, source_target_pairs={{0,16},{8,24},{16,0},{24,8},{1,17},{9,25},{17,1},{25,9},{2,18},{10... | collective-permute-start | bytes 2359304 | tf_op jit(solution)/shard_map/ppermute | solution.py:327
  169.5 0.9 copy-start.3
  173.7 7.7 %collective-permute-start.14 = (bf16[3,512,256]{2,1,0:T(8,128)(2,1)}, bf16[3,512,256]{2,1,0:T(8,128)(2,1)S(1)}, u32[]{:S(2)}, u32[]{:S(2)}) collective-permute-start(bf16[3,512,256]{2,1,0:T(8,128)(2,1)} %get-tuple-element.104.g_own), channel_id=1, source_target_pairs={{0,8},{8,0},{16,24},{24,16},{1,9},{9,1},{17,25},{25,17},{2,10},{10... | collective-permute-start | bytes 2359304 | tf_op jit(solution)/shard_map/ppermute | solution.py:327
  181.5 0.9 copy-start
  202.0 4.9 %copy-start.10 = (f32[3,256,256]{2,1,0:T(8,128)S(1)}, f32[3,256,256]{2,1,0:T(8,128)}, u32[]{:S(2)}) copy-start(f32[3,256,256]{2,1,0:T(8,128)} %get-tuple-element.130) | copy-start | bytes 2359300
  202.0 2.1 collective-permute-start.18
  202.6 4.4 %collective-permute-start.21 = (bf16[3,256,256]{2,1,0:T(8,128)(2,1)}, bf16[3,256,256]{2,1,0:T(8,128)(2,1)S(1)}, u32[]{:S(2)}, u32[]{:S(2)}) collective-permute-start(bf16[3,256,256]{2,1,0:T(8,128)(2,1)} %get-tuple-element.131), channel_id=1, source_target_pairs={{0,8},{8,0},{16,24},{24,16},{1,9},{9,1},{17,25},{25,17},{2,10},{10... | collective-permute-start | bytes 1179656 | tf_op jit(solution)/shard_map/ppermute | solution.py:327
  205.3 11.5 %collective-permute-start.19 = (bf16[3,256,256]{2,1,0:T(8,128)(2,1)S(1)}, bf16[3,256,256]{2,1,0:T(8,128)(2,1)S(1)}, u32[]{:S(2)}, u32[]{:S(2)}) collective-permute-start(bf16[3,256,256]{2,1,0:T(8,128)(2,1)S(1)} %add_convert_fusion.7), channel_id=1, source_target_pairs={{0,16},{8,24},{16,0},{24,8},{1,17},{9,25},{17,1},{25,9},{2,18},{10... | collective-permute-start | bytes 1179656 | tf_op jit(solution)/shard_map/ppermute | solution.py:327
  207.0 11.5 %collective-permute-start.22 = (bf16[3,256,256]{2,1,0:T(8,128)(2,1)S(1)}, bf16[3,256,256]{2,1,0:T(8,128)(2,1)S(1)}, u32[]{:S(2)}, u32[]{:S(2)}) collective-permute-start(bf16[3,256,256]{2,1,0:T(8,128)(2,1)S(1)} %add_convert_fusion.4), channel_id=1, source_target_pairs={{0,1},{1,0},{2,3},{3,2},{4,5},{5,4},{6,7},{7,6},{8,9},{9,8},{10,11... | collective-permute-start | bytes 1179656 | tf_op jit(solution)/shard_map/ppermute | solution.py:327
  216.9 23.2 %collective-permute-start.20 = (bf16[3,256,256]{2,1,0:T(8,128)(2,1)S(1)}, bf16[3,256,256]{2,1,0:T(8,128)(2,1)S(1)}, u32[]{:S(2)}, u32[]{:S(2)}) collective-permute-start(bf16[3,256,256]{2,1,0:T(8,128)(2,1)S(1)} %add_convert_fusion.6), channel_id=1, source_target_pairs={{0,1},{1,0},{2,3},{3,2},{4,5},{5,4},{6,7},{7,6},{8,9},{9,8},{10,11... | collective-permute-start | bytes 1179656 | tf_op jit(solution)/shard_map/ppermute | solution.py:327
  218.6 24.8 %collective-permute-start.23 = (bf16[3,256,256]{2,1,0:T(8,128)(2,1)S(1)}, bf16[3,256,256]{2,1,0:T(8,128)(2,1)S(1)}, u32[]{:S(2)}, u32[]{:S(2)}) collective-permute-start(bf16[3,256,256]{2,1,0:T(8,128)(2,1)S(1)} %add_convert_fusion.3), channel_id=1, source_target_pairs={{0,16},{8,24},{16,0},{24,8},{1,17},{9,25},{17,1},{25,9},{2,18},{10... | collective-permute-start | bytes 1179656 | tf_op jit(solution)/shard_map/ppermute | solution.py:327
  224.3 17.0 %collective-permute-start.9 = (bf16[1,256,512]{2,1,0:T(8,128)(2,1)}, bf16[1,256,512]{2,1,0:T(8,128)(2,1)S(1)}, u32[]{:S(2)}, u32[]{:S(2)}) collective-permute-start(bf16[1,256,512]{2,1,0:T(8,128)(2,1)} %get-tuple-element.97), channel_id=1, source_target_pairs={{0,2},{2,0},{4,6},{6,4},{1,3},{3,1},{5,7},{7,5},{8,10},{10,8},{12,... | collective-permute-start | bytes 786440 | tf_op jit(solution)/shard_map/ppermute | solution.py:327
  224.3 21.3 %collective-permute-start.10 = (bf16[1,256,512]{2,1,0:T(8,128)(2,1)}, bf16[1,256,512]{2,1,0:T(8,128)(2,1)}, u32[]{:S(2)}, u32[]{:S(2)}) collective-permute-start(bf16[1,256,512]{2,1,0:T(8,128)(2,1)} %get-tuple-element.98), channel_id=1, source_target_pairs={{0,4},{2,6},{4,0},{6,2},{1,5},{3,7},{5,1},{7,3},{8,12},{10,14},{12... | collective-permute-start | bytes 786440 | tf_op jit(solution)/shard_map/ppermute | solution.py:327
  227.3 24.8 %collective-permute-start.11 = (bf16[1,256,512]{2,1,0:T(8,128)(2,1)}, bf16[1,256,512]{2,1,0:T(8,128)(2,1)}, u32[]{:S(2)}, u32[]{:S(2)}) collective-permute-start(bf16[1,256,512]{2,1,0:T(8,128)(2,1)} %get-tuple-element.99), channel_id=1, source_target_pairs={{0,6},{2,4},{4,2},{6,0},{1,7},{3,5},{5,3},{7,1},{8,14},{10,12},{12... | collective-permute-start | bytes 786440 | tf_op jit(solution)/shard_map/ppermute | solution.py:327
  240.1 20.9 %collective-permute-start.15 = (bf16[2,256,512]{2,1,0:T(8,128)(2,1)}, bf16[2,256,512]{2,1,0:T(8,128)(2,1)S(1)}, u32[]{:S(2)}, u32[]{:S(2)}) collective-permute-start(bf16[2,256,512]{2,1,0:T(8,128)(2,1)} %get-tuple-element.113), channel_id=1, source_target_pairs={{0,2},{2,0},{4,6},{6,4},{1,3},{3,1},{5,7},{7,5},{8,10},{10,8},{12,... | collective-permute-start | bytes 1572872 | tf_op jit(solution)/shard_map/ppermute | solution.py:327
  241.2 13.2 %copy-start.8 = (bf16[3,256,256]{2,1,0:T(8,128)(2,1)}, bf16[3,256,256]{2,1,0:T(8,128)(2,1)S(1)}, u32[]{:S(2)}) copy-start(bf16[3,256,256]{2,1,0:T(8,128)(2,1)S(1)} %add_convert_fusion.5.refs_0_) | copy-start | bytes 1179652
  241.2 10.9 %copy-start.19 = (bf16[1,256,512]{2,1,0:T(8,128)(2,1)}, bf16[1,256,512]{2,1,0:T(8,128)(2,1)S(1)}, u32[]{:S(2)}) copy-start(bf16[1,256,512]{2,1,0:T(8,128)(2,1)S(1)} %collective-permute-done.9.refs_1_) | copy-start | bytes 786436
  241.3 43.6 %collective-permute-start.16 = (bf16[2,256,512]{2,1,0:T(8,128)(2,1)}, bf16[2,256,512]{2,1,0:T(8,128)(2,1)S(1)}, u32[]{:S(2)}, u32[]{:S(2)}) collective-permute-start(bf16[2,256,512]{2,1,0:T(8,128)(2,1)} %get-tuple-element.114), channel_id=1, source_target_pairs={{0,4},{2,6},{4,0},{6,2},{1,5},{3,7},{5,1},{7,3},{8,12},{10,14},{12... | collective-permute-start | bytes 1572872 | tf_op jit(solution)/shard_map/ppermute | solution.py:327
  243.3 11.0 %copy-start.20 = (f32[1,256,1]{2,1,0:T(8,128)S(1)}, f32[1,256,1]{2,1,0:T(8,128)}, u32[]{:S(2)}) copy-start(f32[1,256,1]{2,1,0:T(8,128)} %get-tuple-element.121) | copy-start | bytes 3076
  243.3 51.4 %collective-permute-start.17 = (bf16[2,256,512]{2,1,0:T(8,128)(2,1)}, bf16[2,256,512]{2,1,0:T(8,128)(2,1)S(1)}, u32[]{:S(2)}, u32[]{:S(2)}) collective-permute-start(bf16[2,256,512]{2,1,0:T(8,128)(2,1)} %get-tuple-element.116), channel_id=1, source_target_pairs={{0,6},{2,4},{4,2},{6,0},{1,7},{3,5},{5,3},{7,1},{8,14},{10,12},{12... | collective-permute-start | bytes 1572872 | tf_op jit(solution)/shard_map/ppermute | solution.py:327
  243.9 54.6 %copy-start.9 = (bf16[3,256,256]{2,1,0:T(8,128)(2,1)}, bf16[3,256,256]{2,1,0:T(8,128)(2,1)S(1)}, u32[]{:S(2)}) copy-start(bf16[3,256,256]{2,1,0:T(8,128)(2,1)S(1)} %add_convert_fusion.2.refs_1_) | copy-start | bytes 1179652
  245.5 53.0 %collective-permute-start.24 = (bf16[3,256,256]{2,1,0:T(8,128)(2,1)S(1)}, bf16[3,256,256]{2,1,0:T(8,128)(2,1)S(1)}, u32[]{:S(2)}, u32[]{:S(2)}) collective-permute-start(bf16[3,256,256]{2,1,0:T(8,128)(2,1)S(1)} %add_convert_fusion.5.refs_0_), channel_id=1, source_target_pairs={{0,8},{8,0},{16,24},{24,16},{1,9},{9,1},{17,25},{25,17},{2,10},{10... | collective-permute-start | bytes 1179656 | tf_op jit(solution)/shard_map/ppermute | solution.py:327
  252.1 46.4 %collective-permute-start.25 = (bf16[3,256,256]{2,1,0:T(8,128)(2,1)S(1)}, bf16[3,256,256]{2,1,0:T(8,128)(2,1)S(1)}, u32[]{:S(2)}, u32[]{:S(2)}) collective-permute-start(bf16[3,256,256]{2,1,0:T(8,128)(2,1)S(1)} %add_convert_fusion.2.refs_1_), channel_id=1, source_target_pairs={{0,8},{8,0},{16,24},{24,16},{1,9},{9,1},{17,25},{25,17},{2,10},{10... | collective-permute-start | bytes 1179656 | tf_op jit(solution)/shard_map/ppermute | solution.py:327
  261.0 33.8 %copy-start.11 = (bf16[2,256,512]{2,1,0:T(8,128)(2,1)}, bf16[2,256,512]{2,1,0:T(8,128)(2,1)S(1)}, u32[]{:S(2)}) copy-start(bf16[2,256,512]{2,1,0:T(8,128)(2,1)S(1)} %collective-permute-done.15.refs_1_) | copy-start | bytes 1572868
  284.9 9.9 %copy-start.12 = (bf16[2,256,512]{2,1,0:T(8,128)(2,1)}, bf16[2,256,512]{2,1,0:T(8,128)(2,1)S(1)}, u32[]{:S(2)}) copy-start(bf16[2,256,512]{2,1,0:T(8,128)(2,1)S(1)} %collective-permute-done.16.refs_2_) | copy-start | bytes 1572868
  294.7 0.8 copy-start.13
  298.5 0.8 copy-start.17
  299.3 0.7 copy-start.18
